TPU v7x, 32 devices: a whole 2x2x4 slice. The times are simulated.
32 devices in a mesh: groups: 2 (over y), tm: 4 (over z), chan: 2 (over x), sub: 2 (over core).
Axes of the slice: x: 2, y: 2, z: 4, core: 2. Of those that a mesh axis runs over, the one named last changes fastest.
Arguments:
- traces: bfloat16 [512, 8192], P(('chan', 'sub'), ('groups', 'tm')), parts along dimension 1, may hold values from -60 to 60
- templates: bfloat16 [32, 512, 256], P('tm', ('chan', 'sub')), may hold values from -6 to 6
- channel_mask: int32 [32, 512], P('tm', ('chan', 'sub')), may hold values from 0 to 1
Outputs:
- scores: float32 [32, 8192], P(('chan', 'sub'), ('groups', 'tm')), parts along dimension 1
There are 2 independent parts, one for each index of `groups`. A program takes and returns all parts, laid end to end along the dimension named above; an argument that names none is the same for every part. Nothing has to cross between parts.
All inputs are finite; a program needn't handle non-finite values.
Results may differ from a plain program's by a relative error of at most 0.0003.
Values may be sent and summed in bfloat16 or wider, within the bound.
No kernel may reach another device: no remote copies, remote signals or barrier semaphores. Data moves between devices by JAX's collectives and lax.ppermute only.
A program may use at most 64 MiB of HBM per device.

v0:
```python
import functools

import jax
import jax.numpy as jnp
from jax import lax
from jax.experimental import pallas as pl
from jax.experimental.pallas import tpu as pltpu
from jax.sharding import PartitionSpec as P


EPSILON = 1e-06
LANE = 128
FRAMES = 4
STEP = LANE // FRAMES
IN_VMEM = pl.BlockSpec(memory_space=pltpu.VMEM)


def shifted(x, axis, by):
    count = lax.axis_size(axis)
    return lax.ppermute(x, axis, [(i, (i + by) % count) for i in range(count)])


def arrange(masked, span):
    rows, chans, _ = masked.shape
    split = masked.reshape(rows, chans, span // LANE, FRAMES, STEP)
    return split.transpose(4, 0, 2, 3, 1).reshape(STEP * rows, span * chans // STEP)


def correlate(weights, signal, frames, partial, rows, width):
    chans = signal.shape[0]
    depth = FRAMES * chans
    blocks = weights.shape[1] // depth
    extent = width + LANE
    reach = extent + (blocks - 1) * LANE
    signal = jnp.concatenate(
        [signal, jnp.zeros((chans, reach + LANE - signal.shape[1]), signal.dtype)], 1
    )
    for frame in range(FRAMES):
        frames[frame * chans : (frame + 1) * chans, :] = signal[:, frame * STEP : frame * STEP + reach]
    total = None
    for block in range(blocks):
        term = jnp.dot(
            weights[:, block * depth : (block + 1) * depth],
            frames[:, block * LANE : block * LANE + extent],
            preferred_element_type=jnp.float32,
        )
        total = term if total is None else total + term
    partial[...] = total
    result = partial[0:rows, 0:width]
    for lag in range(1, STEP):
        result = result + partial[lag * rows : (lag + 1) * rows, lag : lag + width]
    return result


def channel_squares(active, signal):
    wide = signal.astype(jnp.float32)
    squares = wide * wide
    high = squares.astype(jnp.bfloat16)
    low = (squares - high.astype(jnp.float32)).astype(jnp.bfloat16)
    return jnp.dot(
        jnp.concatenate([active, active], 1),
        jnp.concatenate([high, low], 0),
        preferred_element_type=jnp.float32,
    )


def pair_kernel(span, weights, active, first, second, head, corr, squares, frames, partial):
    rows, width = corr.shape
    signal = jnp.concatenate([first[...], second[...], head[:, :span]], 1)
    corr[...] = correlate(weights, signal, frames, partial, rows, width)
    squares[...] = channel_squares(active[...], signal[:, :width])


def pair_scratch(chans, rows, width, span):
    extent = width + LANE
    return [
        pltpu.VMEM((FRAMES * chans, extent + span - LANE), jnp.bfloat16),
        pltpu.VMEM((STEP * rows, extent), jnp.float32),
    ]


def pair_call(weights, active, first, second, head, span):
    rows, chans = active.shape
    width = 2 * first.shape[1]
    shape = jax.ShapeDtypeStruct((rows, width), jnp.float32)
    flops = 2 * weights.shape[0] * weights.shape[1] * (width + LANE)
    return pl.pallas_call(
        functools.partial(pair_kernel, span),
        out_shape=(shape, shape),
        in_specs=[IN_VMEM] * 5,
        out_specs=(IN_VMEM, IN_VMEM),
        scratch_shapes=pair_scratch(chans, rows, width, span),
        cost_estimate=pl.CostEstimate(flops=flops, bytes_accessed=1 << 20, transcendentals=0),
        compiler_params=pltpu.CompilerParams(vmem_limit_bytes=32 << 20),
    )(weights, active, first, second, head)


def early_kernel(span, odd, stats, weights, active, own, near, *refs):
    fars, (corr, energy, wide, edges, squares, frames, partial) = refs[:-7], refs[-7:]
    rows, width = corr.shape
    swap = odd[0] == 1
    far = jnp.concatenate([ref[...] for ref in fars], 1)
    first = jnp.where(swap, far, own[...])
    third = jnp.where(swap, own[...], far)
    signal = jnp.concatenate([first, near[...], third], 1)
    corr[...] = correlate(weights, signal, frames, partial, rows, width)
    sums = channel_squares(active[...], signal)
    energy[...] = line_sums(sums, span)[:, :width]
    edges[:, :span] = signal[:, width:]
    edges[:, span:] = first[:, :span]
    squares[:, :span] = sums[:, width:]
    squares[:, span:] = sums[:, :span]
    wide[...] = jnp.broadcast_to(stats[...], wide.shape)


def early_call(odd, stats, weights, active, own, near, fars, span):
    rows, chans = active.shape
    total = 3 * own.shape[1]
    width = total - span
    flops = 2 * weights.shape[0] * weights.shape[1] * total
    return pl.pallas_call(
        functools.partial(early_kernel, span),
        out_shape=(
            jax.ShapeDtypeStruct((rows, width), jnp.float32),
            jax.ShapeDtypeStruct((rows, width), jnp.float32),
            jax.ShapeDtypeStruct((2 * rows, LANE), jnp.float32),
            jax.ShapeDtypeStruct((chans, 2 * span), own.dtype),
            jax.ShapeDtypeStruct((rows, 2 * span), jnp.float32),
        ),
        in_specs=[pl.BlockSpec(memory_space=pltpu.SMEM)] + [IN_VMEM] * (5 + len(fars)),
        out_specs=(IN_VMEM,) * 5,
        scratch_shapes=pair_scratch(chans, rows, width, span),
        cost_estimate=pl.CostEstimate(flops=flops, bytes_accessed=1 << 20, transcendentals=0),
        compiler_params=pltpu.CompilerParams(vmem_limit_bytes=32 << 20),
    )(odd, stats, weights, active, own, near, *fars)


def middle_kernel(span, weights, active, part, edges, squares, corr, energy, tail, frames, partial):
    rows, width = corr.shape
    signal = jnp.concatenate([edges[:, :span], part[...]], 1)
    sums = channel_squares(active[...], part[...])
    tail[...] = sums[:, width - span :]
    sums = jnp.concatenate([squares[:, :span], sums], 1)
    energy[...] = line_sums(sums, span)[:, :width]
    corr[...] = correlate(weights, signal, frames, partial, rows, width)


def middle_call(weights, active, part, edges, squares, span):
    rows, chans = active.shape
    width = part.shape[1]
    flops = 2 * weights.shape[0] * weights.shape[1] * width
    shape = jax.ShapeDtypeStruct((rows, width), jnp.float32)
    return pl.pallas_call(
        functools.partial(middle_kernel, span),
        out_shape=(shape, shape, jax.ShapeDtypeStruct((rows, span), jnp.float32)),
        in_specs=[IN_VMEM] * 5,
        out_specs=(IN_VMEM,) * 3,
        scratch_shapes=pair_scratch(chans, rows, width, span),
        cost_estimate=pl.CostEstimate(flops=flops, bytes_accessed=1 << 20, transcendentals=0),
        compiler_params=pltpu.CompilerParams(vmem_limit_bytes=32 << 20),
    )(weights, active, part, edges, squares)


def late_kernel(span, ways, place, order, weights, active, before, part, corr, energy, stats, edges, squares, middle_corr, middle_energy, tail, *refs):
    outs, (corr_all, energy_all, frames, partial) = refs[:ways], refs[ways:]
    rows, total = corr_all.shape
    early, done = corr.shape[1], corr.shape[1] + middle_corr.shape[1]
    signal = jnp.concatenate([before[:, before.shape[1] - span :], part[...], edges[:, span:]], 1)
    sums = channel_squares(active[...], part[...])
    sums = jnp.concatenate([tail[...], sums, squares[:, span:]], 1)
    energy_all[:, :early] = energy[...]
    energy_all[:, early:done] = middle_energy[...]
    energy_all[:, done:] = line_sums(sums, span)[:, : total - done]
    corr_all[:, :early] = corr[...]
    corr_all[:, early:done] = middle_corr[...]
    corr_all[:, done:] = correlate(weights, signal, frames, partial, rows, total - done)
    share(place, order, total // order.shape[0], corr_all, energy_all, stats, outs)


def late_call(place, order, weights, active, before, part, early, middle, span, ways):
    rows = active.shape[0]
    chans, width = part.shape
    total = early[0].shape[1] + middle[0].shape[1] + span + width
    shape = jax.ShapeDtypeStruct((2 * rows, total // ways + LANE), jnp.float32)
    flops = 2 * weights.shape[0] * weights.shape[1] * (width + span)
    return pl.pallas_call(
        functools.partial(late_kernel, span, ways),
        out_shape=(shape,) * ways,
        in_specs=[pl.BlockSpec(memory_space=pltpu.SMEM)] * 2 + [IN_VMEM] * (4 + len(early) + len(middle)),
        out_specs=(IN_VMEM,) * ways,
        scratch_shapes=[pltpu.VMEM((rows, total), jnp.float32)] * 2
        + pair_scratch(chans, rows, width + span, span),
        cost_estimate=pl.CostEstimate(flops=flops, bytes_accessed=1 << 20, transcendentals=0),
        compiler_params=pltpu.CompilerParams(vmem_limit_bytes=32 << 20),
    )(place, order, weights, active, before, part, *early, *middle)


def share(place, order, tile, corr_all, energy_all, stats, outs):
    rows, total = corr_all.shape
    ways = len(outs)
    count = total // tile // ways
    for shift in range(ways):
        group = lax.rem(place[0] + shift, ways) * count
        for item in range(count):
            start = pl.multiple_of(order[group + item] * tile, LANE)
            columns = slice(item * tile, (item + 1) * tile)
            outs[shift][0:rows, columns] = corr_all[:, pl.ds(start, tile)]
            outs[shift][rows : 2 * rows, columns] = energy_all[:, pl.ds(start, tile)]
        outs[shift][:, count * tile :] = stats[...]


def line_sums(values, span):
    reach = 1
    while reach < span:
        values = values + jnp.concatenate([values[:, reach:], values[:, :reach]], 1)
        reach *= 2
    return values


def pack_kernel(span, tile, pairs, place, order, stats, *refs):
    corrs, squares = refs[:pairs], refs[pairs : 2 * pairs]
    outs, corr_all, energy_all = refs[2 * pairs : -2], refs[-2], refs[-1]
    corr = jnp.concatenate([ref[...] for ref in corrs], 1)
    corr_all[...] = jnp.concatenate([corr[:, tile:], corr[:, :tile]], 1)
    energy = line_sums(jnp.concatenate([ref[...] for ref in squares], 1), span)
    energy_all[...] = jnp.concatenate([energy[:, tile:], energy[:, :tile]], 1)
    share(place, order, tile, corr_all, energy_all, stats, outs)


def pack_call(place, order, stats, corrs, squares, span, ways):
    rows, width = corrs[0].shape
    pairs = len(corrs)
    total = pairs * width
    shape = jax.ShapeDtypeStruct((2 * rows, total // ways + LANE), jnp.float32)
    return pl.pallas_call(
        functools.partial(pack_kernel, span, width // 2, pairs),
        out_shape=(shape,) * ways,
        in_specs=[pl.BlockSpec(memory_space=pltpu.SMEM)] * 2 + [IN_VMEM] * (1 + 2 * pairs),
        out_specs=(IN_VMEM,) * ways,
        scratch_shapes=[pltpu.VMEM((rows, total), jnp.float32)] * 2,
        compiler_params=pltpu.CompilerParams(vmem_limit_bytes=16 << 20),
    )(place, order, stats, *corrs, *squares)


def split_kernel(ways, count, place, *refs):
    ins, outs, held = refs[:count], refs[count:-1], refs[-1]
    total = ins[0][...]
    for ref in ins[1:]:
        total = total + ref[...]
    held[...] = total
    part = (held.shape[1] - LANE) // ways
    for shift in range(ways):
        start = pl.multiple_of(lax.rem(place[0] + shift, ways) * part, LANE)
        outs[shift][:, 0:part] = held[:, pl.ds(start, part)]
        outs[shift][:, part:] = held[:, part * ways :]


def split_call(place, parts, ways):
    rows, width = parts[0].shape
    shape = jax.ShapeDtypeStruct((rows, (width - LANE) // ways + LANE), jnp.float32)
    return pl.pallas_call(
        functools.partial(split_kernel, ways, len(parts)),
        out_shape=(shape,) * ways,
        in_specs=[pl.BlockSpec(memory_space=pltpu.SMEM)] + [IN_VMEM] * len(parts),
        out_specs=(IN_VMEM,) * ways,
        scratch_shapes=[pltpu.VMEM((rows, width), jnp.float32)],
        compiler_params=pltpu.CompilerParams(vmem_limit_bytes=16 << 20),
    )(place, *parts)


def score_kernel(span, count, *refs):
    ins, out = refs[:count], refs[count]
    total = ins[0][...]
    for ref in ins[1:]:
        total = total + ref[...]
    rows, width = out.shape
    template_energy = total[0:rows, width : width + 1]
    active_count = total[rows:, width : width + 1]
    factor = jnp.sqrt(span * active_count)
    energy = total[rows:, 0:width]
    out[...] = total[0:rows, 0:width] * factor / jnp.sqrt(energy * template_energy + EPSILON)


def score_call(parts, span):
    rows, width = parts[0].shape
    return pl.pallas_call(
        functools.partial(score_kernel, span, len(parts)),
        out_shape=jax.ShapeDtypeStruct((rows // 2, width - LANE), jnp.float32),
        in_specs=[IN_VMEM] * len(parts),
        out_specs=IN_VMEM,
        compiler_params=pltpu.CompilerParams(vmem_limit_bytes=16 << 20),
    )(*parts)


def exchange(parts, axis):
    return [parts[0]] + [shifted(part, axis, shift) for shift, part in enumerate(parts) if shift]


def paired(x, axis, bit):
    return lax.ppermute(x, axis, [(i, i ^ bit) for i in range(lax.axis_size(axis))])


def relays(circle, ways):
    return circle == ways == 4


def relayed_sums(traces, weights, active, stats, sub_place, order, span, ways):
    half = traces.shape[1] // 2
    fars = [paired(traces[:, :half], "tm", 2)]
    fars.append(paired(traces[:, half:], "tm", 2))
    near = paired(traces, "tm", 1)
    before, part = [paired(far, "tm", 1) for far in fars]
    odd = (lax.axis_index("tm") % 2).astype(jnp.int32)[None]
    early = early_call(odd, stats, weights, active, traces, near, fars, span)
    middle = middle_call(weights, active, before, early[3], early[4], span)
    return late_call(sub_place, order, weights, active, before, part, early, middle, span, ways)


def routes(circle, chan_ways, sub_ways):
    held = circle // (chan_ways * sub_ways)
    table = []
    for place in range(circle):
        chan, sub = divmod(place // held, sub_ways)
        slots = [(s, c, h) for s in range(sub_ways) for c in range(chan_ways) for h in range(held)]
        tiles = sorted(range(circle), key=lambda t: -abs(t - place))
        ranked = sorted(range(circle), key=lambda k: (slots[k][1] != chan, slots[k][0] == sub))
        row = [0] * circle
        for slot, time_tile in zip(ranked, tiles):
            row[slot] = time_tile
        table.append(row)
    return table


def gathered_sums(traces, weights, active, stats, sub_place, order, span, ways):
    circle = lax.axis_size("tm")
    arrived = {0: traces}
    for hop in range(1, circle // 2 + 1):
        for near in dict.fromkeys((hop, circle - hop)):
            arrived[near] = shifted(traces, "tm", -near)
    corrs, squares = [], []
    for pair in range(circle // 2):
        first, second = arrived[(2 * pair - 1) % circle], arrived[2 * pair]
        head = arrived[(2 * pair + 1) % circle]
        corr, square = pair_call(weights, active, first, second, head, span)
        corrs.append(corr)
        squares.append(square)
    stats = jnp.broadcast_to(stats, (stats.shape[0], LANE))
    return pack_call(sub_place, order, stats, corrs, squares, span, ways)


def on_device(traces, templates, channel_mask):
    tile = traces.shape[1]
    rows, _, span = templates.shape
    circle = lax.axis_size("tm")
    chan_ways, sub_ways = lax.axis_size("chan"), lax.axis_size("sub")
    active = channel_mask.astype(jnp.bfloat16)
    masked = templates * active[:, :, None]
    weights = arrange(masked, span)
    wide = masked.astype(jnp.float32)
    template_energy = jnp.sum(wide * wide, axis=(1, 2))
    active_count = jnp.sum(channel_mask, axis=1).astype(jnp.float32)
    stats = jnp.concatenate([template_energy, active_count])[:, None]
    sub_place = lax.axis_index("sub").astype(jnp.int32)[None]
    chan_place = lax.axis_index("chan").astype(jnp.int32)[None]

    ways = chan_ways * sub_ways
    held = circle // ways
    relayed = relays(circle, ways)
    if relayed:
        table = routes(circle, chan_ways, sub_ways)
        order = (jnp.array(table, jnp.int32)[lax.axis_index("tm")] + lax.axis_index("tm")) % circle
    else:
        table = [[(slot + place) % circle for slot in range(circle)] for place in range(circle)]
        order = jnp.arange(circle, dtype=jnp.int32)
    sums = relayed_sums if relayed else gathered_sums
    parts = sums(traces, weights, active, stats, sub_place, order.astype(jnp.int32), span, sub_ways)
    parts = exchange(parts, "sub")
    parts = exchange(split_call(chan_place, parts, chan_ways), "chan")
    scores = score_call(parts, span)

    received = []
    for piece in range(held):
        pairs = []
        for place in range(circle):
            for chan in range(chan_ways):
                for sub in range(sub_ways):
                    source = (place * chan_ways + chan) * sub_ways + sub
                    slot = (sub * chan_ways + chan) * held + piece
                    pairs.append((source, table[place][slot] * ways + place // held))
        block = scores[:, piece * tile : (piece + 1) * tile]
        received.append(lax.ppermute(block, ("tm", "chan", "sub"), pairs))
    if held == 1:
        return received[0]
    turn = (lax.axis_index("tm") - jnp.arange(held)) % held
    return jnp.stack(received)[turn].reshape(held * rows, tile)


def solution(mesh):
    placed = (
        P(("chan", "sub"), ("groups", "tm")),
        P("tm", ("chan", "sub"), None),
        P("tm", ("chan", "sub")),
    )
    return jax.shard_map(
        on_device,
        mesh=mesh,
        in_specs=placed,
        out_specs=P(("chan", "sub"), ("groups", "tm")),
        check_vma=False,
    )
```

profile of v0, /device:TPU:0, one launch (start us, length us, event | category | flops | bytes accessed | tf_op | source)
XLA Modules:
  0.0 35.5 jit_solution(7628463585178892762)
XLA Ops:
  0.0 0.0 copy-start.1
  0.0 3.1 %collective-permute-start.4 = (bf16[128,1024]{1,0:T(8,128)(2,1)}, bf16[128,1024]{1,0:T(8,128)(2,1)S(1)}, u32[]{:S(2)}, u32[]{:S(2)}) collective-permute-start(bf16[128,1024]{1,0:T(8,128)(2,1)} %own.1), channel_id=1, source_target_pairs={{0,4},{4,0},{8,12},{12,8},{1,5},{5,1},{9,13},{13,9},{2,6},{6,2},{1... | collective-permute-start | bytes 786440 | tf_op jit(solution)/shard_map/ppermute | solution.py:300
  3.1 1.0 %fusion.1 = (bf16[128,512]{1,0:T(8,128)(2,1)S(1)}, bf16[128,512]{1,0:T(8,128)(2,1)S(1)}) fusion(bf16[128,1024]{1,0:T(8,128)(2,1)} %own.1), kind=kLoop, calls=%fused_computation.7 | loop fusion | bytes 524288 | tf_op jit(solution)/shard_map/slice | solution.py:310
  4.1 2.7 %collective-permute-start = (bf16[128,512]{1,0:T(8,128)(2,1)S(1)}, bf16[128,512]{1,0:T(8,128)(2,1)S(1)}, u32[]{:S(2)}, u32[]{:S(2)}) collective-permute-start(bf16[128,512]{1,0:T(8,128)(2,1)S(1)} %get-tuple-element.32), channel_id=1, source_target_pairs={{0,8},{4,12},{8,0},{12,4},{1,9},{5,13},{9,1},{13,5},{2,10},{6,14},... | collective-permute-start | bytes 393224 | tf_op jit(solution)/shard_map/ppermute | solution.py:300
  6.7 0.3 collective-permute-start.2
  7.0 0.9 %fusion.2 = (s32[8]{0:T(128)S(1)}, bf16[8,128]{1,0:T(8,128)(2,1)S(1)}) fusion(s32[8,128]{1,0:T(8,128)} %param.6), kind=kLoop, calls=%fused_computation.8 | loop fusion | flops 2040 | bytes 6176 | tf_op jit(solution)/shard_map/reduce_sum | solution.py:361
  7.9 0.0 copy-done.1
  7.9 0.3 copy.7
  8.2 0.3 multiply_reduce_fusion
  8.5 0.1 maximum_bitcast_fusion
  8.6 0.3 copy.8
  8.9 0.1 copy.9.stats
  9.0 0.7 %and_select_fusion.order = s32[4]{0:T(128)S(1)} fusion(s32[4,4]{1,0:T(4,128)} %constant.43.clone, s32[]{:T(128)S(6)} %select_n.16, s32[]{:T(128)S(6)} %axis_index.46), kind=kLoop, calls=%fused_computation.4 | loop fusion | flops 48 | bytes 40 | tf_op jit(solution)/shard_map/jit(remainder)/select_n | solution.py:371
  9.7 3.1 %collective-permute-done.refs_0_ = bf16[128,512]{1,0:T(8,128)(2,1)S(1)} collective-permute-done((bf16[128,512]{1,0:T(8,128)(2,1)S(1)}, bf16[128,512]{1,0:T(8,128)(2,1)S(1)}, u32[]{:S(2)}, u32[]{:S(2)}) %collective-permute-start) | collective-permute-done | bytes 131104 | tf_op jit(solution)/shard_map/ppermute | solution.py:300
  12.8 3.7 %collective-permute-start.1 = (bf16[128,512]{1,0:T(8,128)(2,1)S(1)}, bf16[128,512]{1,0:T(8,128)(2,1)S(1)}, u32[]{:S(2)}, u32[]{:S(2)}) collective-permute-start(bf16[128,512]{1,0:T(8,128)(2,1)S(1)} %collective-permute-done.refs_0_), channel_id=1, source_target_pairs={{0,4},{4,0},{8,12},{12,8},{1,5},{5,1},{9,13},{13,9},{2,6},{6,2},{1... | collective-permute-start | bytes 393224 | tf_op jit(solution)/shard_map/ppermute | solution.py:300
  16.5 1.8 %collective-permute-done.2.refs_1_ = bf16[128,512]{1,0:T(8,128)(2,1)S(1)} collective-permute-done((bf16[128,512]{1,0:T(8,128)(2,1)S(1)}, bf16[128,512]{1,0:T(8,128)(2,1)S(1)}, u32[]{:S(2)}, u32[]{:S(2)}) %collective-permute-start.2) | collective-permute-done | bytes 131104 | tf_op jit(solution)/shard_map/ppermute | solution.py:300
  18.3 0.8 %collective-permute-start.3 = (bf16[128,512]{1,0:T(8,128)(2,1)S(1)}, bf16[128,512]{1,0:T(8,128)(2,1)S(1)}, u32[]{:S(2)}, u32[]{:S(2)}) collective-permute-start(bf16[128,512]{1,0:T(8,128)(2,1)S(1)} %collective-permute-done.2.refs_1_), channel_id=1, source_target_pairs={{0,4},{4,0},{8,12},{12,8},{1,5},{5,1},{9,13},{13,9},{2,6},{6,2},{1... | collective-permute-start | bytes 393224 | tf_op jit(solution)/shard_map/ppermute | solution.py:300
  19.1 0.0 collective-permute-done.4.near
  19.1 0.0 copy-done
  19.1 2.9 %shard_map.46 = (f32[8,2816]{1,0:T(8,128)S(1)}, f32[8,2816]{1,0:T(8,128)S(1)}, f32[16,128]{1,0:T(8,128)S(1)}, bf16[128,512]{1,0:T(8,128)(2,1)S(1)}, f32[8,512]{1,0:T(8,128)S(1)}) custom-call(s32[1]{0:T(128)} %bitcast.6.odd, f32[16,1]{1,0:T(8,128)S(1)} %copy.9.stats, bf16[256,1024]{1,0:T(8,128)(2,1)S(1)} %bitcast.11, ...), custom_call_target="tpu_custom_call" | custom-call | flops 1610612736 | bytes 1048576 | tf_op jit(solution)/shard_map/pallas_call | solution.py:121
  22.0 0.0 collective-permute-done.1.part.before
  22.0 0.9 %shard_map.47 = (f32[8,512]{1,0:T(8,128)S(1)}, f32[8,512]{1,0:T(8,128)S(1)}, f32[8,256]{1,0:T(8,128)S(1)}) custom-call(bf16[256,1024]{1,0:T(8,128)(2,1)S(1)} %bitcast.12, bf16[8,128]{1,0:T(8,128)(2,1)S(1)} %get-tuple-element.34.active, bf16[128,512]{1,0:T(8,128)(2,1)S(1)} %collective-permute-done.1.part.before, ...), custom_call_target="tpu_custom_call" | custom-call | flops 268435456 | bytes 1048576 | tf_op jit(solution)/shard_map/pallas_call | solution.py:153
  22.9 0.4 %collective-permute-done.3.part = bf16[128,512]{1,0:T(8,128)(2,1)S(1)} collective-permute-done((bf16[128,512]{1,0:T(8,128)(2,1)S(1)}, bf16[128,512]{1,0:T(8,128)(2,1)S(1)}, u32[]{:S(2)}, u32[]{:S(2)}) %collective-permute-start.3) | collective-permute-done | bytes 131104 | tf_op jit(solution)/shard_map/ppermute | solution.py:300
  23.3 1.7 %shard_map.48 = (f32[16,2176]{1,0:T(8,128)S(1)}, f32[16,2176]{1,0:T(8,128)S(1)}) custom-call(s32[1]{0:T(128)} %bitcast.1.place, s32[4]{0:T(128)S(1)} %and_select_fusion.order, bf16[256,1024]{1,0:T(8,128)(2,1)S(1)} %bitcast.13, bf16[8,128]{1,0:T(8,128)(2,1)S(1)} %get-tuple-element.34.active, bf16[128,512]{1,0:T(8,128)(2,1)S(1)} %collective-permute-done.1.part.before, ...), custom_call_target="tpu_custom_call" | custom-call | flops 402653184 | bytes 1048576 | tf_op jit(solution)/shard_map/pallas_call | solution.py:186
  25.0 0.1 collective-permute-start.5
  25.0 1.3 %collective-permute-done.5.refs_1_ = f32[16,2176]{1,0:T(8,128)S(1)} collective-permute-done((f32[16,2176]{1,0:T(8,128)S(1)}, f32[16,2176]{1,0:T(8,128)S(1)}, u32[]{:S(2)}, u32[]{:S(2)}) %collective-permute-start.5) | collective-permute-done | bytes 139296 | tf_op jit(solution)/shard_map/ppermute | solution.py:20
  26.4 1.6 %collective-permute-start.6 = (f32[16,1152]{1,0:T(8,128)S(1)}, f32[16,1152]{1,0:T(8,128)S(1)}, u32[]{:S(2)}, u32[]{:S(2)}) collective-permute-start(f32[16,1152]{1,0:T(8,128)S(1)} %get-tuple-element.28), channel_id=1, source_target_pairs={{0,2},{2,0},{1,3},{3,1},{4,6},{6,4},{5,7},{7,5},{8,10},{10,8},{9,1... | collective-permute-start | bytes 221192 | tf_op jit(solution)/shard_map/ppermute | solution.py:20
  28.0 2.9 %collective-permute-done.6.refs_1_ = f32[16,1152]{1,0:T(8,128)S(1)} collective-permute-done((f32[16,1152]{1,0:T(8,128)S(1)}, f32[16,1152]{1,0:T(8,128)S(1)}, u32[]{:S(2)}, u32[]{:S(2)}) %collective-permute-start.6) | collective-permute-done | bytes 73760 | tf_op jit(solution)/shard_map/ppermute | solution.py:20
  30.8 0.1 shard_map.50
  30.9 2.1 %collective-permute-start.7 = (f32[8,1024]{1,0:T(8,128)S(1)}, f32[8,1024]{1,0:T(8,128)S(1)}, u32[]{:S(2)}, u32[]{:S(2)}) collective-permute-start(f32[8,1024]{1,0:T(8,128)S(1)} %shard_map.50), channel_id=1, source_target_pairs={{0,8},{1,12},{2,0},{3,4},{4,13},{5,1},{6,9},{7,5},{8,10},{9,14},{1... | collective-permute-start | bytes 98312 | tf_op jit(solution)/shard_map/ppermute | solution.py:391
  33.0 1.9 %collective-permute-done.7 = f32[8,1024]{1,0:T(8,128)S(1)} collective-permute-done((f32[8,1024]{1,0:T(8,128)S(1)}, f32[8,1024]{1,0:T(8,128)S(1)}, u32[]{:S(2)}, u32[]{:S(2)}) %collective-permute-start.7) | collective-permute-done | bytes 32800 | tf_op jit(solution)/shard_map/ppermute | solution.py:391
  34.9 0.6 %copy.11 = f32[8,1024]{1,0:T(8,128)} copy(f32[8,1024]{1,0:T(8,128)S(1)} %collective-permute-done.7) | data formatting | bytes 65536
  (3 shorter events, 0.0 us)
Async XLA Ops:
  0.0 7.9 %copy-start.1 = (bf16[8,128,256]{2,1,0:T(8,128)(2,1)S(1)}, bf16[8,128,256]{2,1,0:T(8,128)(2,1)}, u32[]{:S(2)}) copy-start(bf16[8,128,256]{2,1,0:T(8,128)(2,1)} %param.5) | copy-start | bytes 1572868
  0.0 19.1 %collective-permute-start.4 = (bf16[128,1024]{1,0:T(8,128)(2,1)}, bf16[128,1024]{1,0:T(8,128)(2,1)S(1)}, u32[]{:S(2)}, u32[]{:S(2)}) collective-permute-start(bf16[128,1024]{1,0:T(8,128)(2,1)} %own.1), channel_id=1, source_target_pairs={{0,4},{4,0},{8,12},{12,8},{1,5},{5,1},{9,13},{13,9},{2,6},{6,2},{1... | collective-permute-start | bytes 786440 | tf_op jit(solution)/shard_map/ppermute | solution.py:300
  4.1 8.8 %collective-permute-start = (bf16[128,512]{1,0:T(8,128)(2,1)S(1)}, bf16[128,512]{1,0:T(8,128)(2,1)S(1)}, u32[]{:S(2)}, u32[]{:S(2)}) collective-permute-start(bf16[128,512]{1,0:T(8,128)(2,1)S(1)} %get-tuple-element.32), channel_id=1, source_target_pairs={{0,8},{4,12},{8,0},{12,4},{1,9},{5,13},{9,1},{13,5},{2,10},{6,14},... | collective-permute-start | bytes 393224 | tf_op jit(solution)/shard_map/ppermute | solution.py:300
  6.7 11.6 %collective-permute-start.2 = (bf16[128,512]{1,0:T(8,128)(2,1)S(1)}, bf16[128,512]{1,0:T(8,128)(2,1)S(1)}, u32[]{:S(2)}, u32[]{:S(2)}) collective-permute-start(bf16[128,512]{1,0:T(8,128)(2,1)S(1)} %get-tuple-element.31), channel_id=1, source_target_pairs={{0,8},{4,12},{8,0},{12,4},{1,9},{5,13},{9,1},{13,5},{2,10},{6,14},... | collective-permute-start | bytes 393224 | tf_op jit(solution)/shard_map/ppermute | solution.py:300
  8.6 10.6 %copy-start = (bf16[128,1024]{1,0:T(8,128)(2,1)S(1)}, bf16[128,1024]{1,0:T(8,128)(2,1)}, u32[]{:S(2)}) copy-start(bf16[128,1024]{1,0:T(8,128)(2,1)} %own.1) | copy-start | bytes 786436
  12.8 9.2 %collective-permute-start.1 = (bf16[128,512]{1,0:T(8,128)(2,1)S(1)}, bf16[128,512]{1,0:T(8,128)(2,1)S(1)}, u32[]{:S(2)}, u32[]{:S(2)}) collective-permute-start(bf16[128,512]{1,0:T(8,128)(2,1)S(1)} %collective-permute-done.refs_0_), channel_id=1, source_target_pairs={{0,4},{4,0},{8,12},{12,8},{1,5},{5,1},{9,13},{13,9},{2,6},{6,2},{1... | collective-permute-start | bytes 393224 | tf_op jit(solution)/shard_map/ppermute | solution.py:300
  18.3 5.0 %collective-permute-start.3 = (bf16[128,512]{1,0:T(8,128)(2,1)S(1)}, bf16[128,512]{1,0:T(8,128)(2,1)S(1)}, u32[]{:S(2)}, u32[]{:S(2)}) collective-permute-start(bf16[128,512]{1,0:T(8,128)(2,1)S(1)} %collective-permute-done.2.refs_1_), channel_id=1, source_target_pairs={{0,4},{4,0},{8,12},{12,8},{1,5},{5,1},{9,13},{13,9},{2,6},{6,2},{1... | collective-permute-start | bytes 393224 | tf_op jit(solution)/shard_map/ppermute | solution.py:300
  25.0 1.4 %collective-permute-start.5 = (f32[16,2176]{1,0:T(8,128)S(1)}, f32[16,2176]{1,0:T(8,128)S(1)}, u32[]{:S(2)}, u32[]{:S(2)}) collective-permute-start(f32[16,2176]{1,0:T(8,128)S(1)} %get-tuple-element.26), channel_id=1, source_target_pairs={{0,1},{1,0},{2,3},{3,2},{4,5},{5,4},{6,7},{7,6},{8,9},{9,8},{10,11... | collective-permute-start | bytes 417800 | tf_op jit(solution)/shard_map/ppermute | solution.py:20
  26.4 4.4 %collective-permute-start.6 = (f32[16,1152]{1,0:T(8,128)S(1)}, f32[16,1152]{1,0:T(8,128)S(1)}, u32[]{:S(2)}, u32[]{:S(2)}) collective-permute-start(f32[16,1152]{1,0:T(8,128)S(1)} %get-tuple-element.28), channel_id=1, source_target_pairs={{0,2},{2,0},{1,3},{3,1},{4,6},{6,4},{5,7},{7,5},{8,10},{10,8},{9,1... | collective-permute-start | bytes 221192 | tf_op jit(solution)/shard_map/ppermute | solution.py:20
  30.9 4.0 %collective-permute-start.7 = (f32[8,1024]{1,0:T(8,128)S(1)}, f32[8,1024]{1,0:T(8,128)S(1)}, u32[]{:S(2)}, u32[]{:S(2)}) collective-permute-start(f32[8,1024]{1,0:T(8,128)S(1)} %shard_map.50), channel_id=1, source_target_pairs={{0,8},{1,12},{2,0},{3,4},{4,13},{5,1},{6,9},{7,5},{8,10},{9,14},{1... | collective-permute-start | bytes 98312 | tf_op jit(solution)/shard_map/ppermute | solution.py:391
where the time goes:
time: 35.7 us; the launch traced here: 35.5 us
  starting transfers between devices  14.3 us (40%)
  waiting for transfers between devices  11.4 us (32%)
  Pallas kernels  5.56 us (16%)
  local copies, waits for them, and re-layouts  2.32 us (6%)
  other arithmetic  1.93 us (5%)
    ppermute x5, starting transfers between devices, paired(): lax.ppermute(x, axis, [(i, i ^ bit) for i in range(lax.axis_size(axis))])  10.5 us
    ppermute x5, waiting for transfers between devices, paired(): lax.ppermute(x, axis, [(i, i ^ bit) for i in range(lax.axis_size(axis))])  5.29 us
    ppermute x2, waiting for transfers between devices, shifted(): return lax.ppermute(x, axis, [(i, (i + by) % count) for i in range(count)])  4.2 us
    pallas_call x1, Pallas kernels, early_call(): pl.pallas_call(functools.partial(early_kernel, span), out_shape=(jax.Shap...  2.9 us
    ppermute x1, starting transfers between devices, on_device(): received.append(lax.ppermute(block, ('tm', 'chan', 'sub'), pairs))  2.08 us
    ppermute x1, waiting for transfers between devices, on_device(): received.append(lax.ppermute(block, ('tm', 'chan', 'sub'), pairs))  1.89 us
    pallas_call x1, Pallas kernels, late_call(): pl.pallas_call(functools.partial(late_kernel, span, ways), out_shape=(sha...  1.66 us
    ppermute x2, starting transfers between devices, shifted(): return lax.ppermute(x, axis, [(i, (i + by) % count) for i in range(count)])  1.63 us
  transfers between devices with their start and end apart: 8, of which 6 were waited for; matrix products, arithmetic and copies ran while one was open for 10% of the time, Pallas kernels for 11%

commit v1 on v0

v1 whole, which is shorter than its diff:
```python
import functools

import jax
import jax.numpy as jnp
from jax import lax
from jax.experimental import pallas as pl
from jax.experimental.pallas import tpu as pltpu
from jax.sharding import PartitionSpec as P


EPSILON = 1e-06
LANE = 128
FRAMES = 4
STEP = LANE // FRAMES
IN_VMEM = pl.BlockSpec(memory_space=pltpu.VMEM)


def shifted(x, axis, by):
    count = lax.axis_size(axis)
    return lax.ppermute(x, axis, [(i, (i + by) % count) for i in range(count)])


def arrange(masked, span):
    rows, chans, _ = masked.shape
    split = masked.reshape(rows, chans, span // LANE, FRAMES, STEP)
    return split.transpose(2, 4, 0, 3, 1).reshape(span * rows // FRAMES, FRAMES * chans)


def correlate(weights, signal, frames, partial, rows, width):
    chans = signal.shape[0]
    depth = STEP * rows
    blocks = weights.shape[0] // depth
    extent = width + LANE
    reach = extent + (blocks - 1) * LANE
    signal = jnp.concatenate(
        [signal, jnp.zeros((chans, reach + LANE - signal.shape[1]), signal.dtype)], 1
    )
    for frame in range(FRAMES):
        frames[frame * chans : (frame + 1) * chans, :] = signal[:, frame * STEP : frame * STEP + reach]
    total = None
    for block in range(blocks):
        term = jnp.dot(
            weights[block * depth : (block + 1) * depth, :],
            frames[:, block * LANE : block * LANE + extent],
            preferred_element_type=jnp.float32,
        )
        total = term if total is None else total + term
    partial[...] = total
    result = partial[0:rows, 0:width]
    for lag in range(1, STEP):
        result = result + partial[lag * rows : (lag + 1) * rows, lag : lag + width]
    return result


def correlate_alone(weights, part, frames, partial, rows):
    chans, width = part.shape
    depth = STEP * rows
    blocks = weights.shape[0] // depth
    extent = width + LANE
    gap = jnp.zeros((chans, LANE), part.dtype)
    signal = jnp.concatenate([gap, part, gap], 1)
    for frame in range(FRAMES):
        frames[frame * chans : (frame + 1) * chans, :] = signal[:, frame * STEP : frame * STEP + extent]
    partial[...] = jnp.dot(weights[...], frames[...], preferred_element_type=jnp.float32)
    span = blocks * LANE
    result = None
    for lag in range(STEP):
        row = None
        for block in range(blocks):
            first = block * depth + lag * rows
            ends = span - LANE - block * LANE, block * LANE
            pieces = [partial[first : first + rows, :]]
            if ends[0]:
                pieces.insert(0, jnp.zeros((rows, ends[0]), jnp.float32))
            if ends[1]:
                pieces.append(jnp.zeros((rows, ends[1]), jnp.float32))
            piece = jnp.concatenate(pieces, 1)
            row = piece if row is None else row + piece
        row = pltpu.roll(row, span + width - lag, 1) if lag else row
        result = row if result is None else result + row
    return result


def channel_squares(active, signal):
    wide = signal.astype(jnp.float32)
    squares = wide * wide
    high = squares.astype(jnp.bfloat16)
    low = (squares - high.astype(jnp.float32)).astype(jnp.bfloat16)
    return jnp.dot(
        jnp.concatenate([active, active], 1),
        jnp.concatenate([high, low], 0),
        preferred_element_type=jnp.float32,
    )


def pair_kernel(span, weights, active, first, second, head, corr, squares, frames, partial):
    rows, width = corr.shape
    signal = jnp.concatenate([first[...], second[...], head[:, :span]], 1)
    corr[...] = correlate(weights, signal, frames, partial, rows, width)
    squares[...] = channel_squares(active[...], signal[:, :width])


def pair_scratch(chans, rows, width, span):
    extent = width + LANE
    return [
        pltpu.VMEM((FRAMES * chans, extent + span - LANE), jnp.bfloat16),
        pltpu.VMEM((STEP * rows, extent), jnp.float32),
    ]


def pair_call(weights, active, first, second, head, span):
    rows, chans = active.shape
    width = 2 * first.shape[1]
    shape = jax.ShapeDtypeStruct((rows, width), jnp.float32)
    flops = 2 * weights.shape[0] * weights.shape[1] * (width + LANE)
    return pl.pallas_call(
        functools.partial(pair_kernel, span),
        out_shape=(shape, shape),
        in_specs=[IN_VMEM] * 5,
        out_specs=(IN_VMEM, IN_VMEM),
        scratch_shapes=pair_scratch(chans, rows, width, span),
        cost_estimate=pl.CostEstimate(flops=flops, bytes_accessed=1 << 20, transcendentals=0),
        compiler_params=pltpu.CompilerParams(vmem_limit_bytes=32 << 20),
    )(weights, active, first, second, head)


def outer_kernel(span, odd, weights, active, own, *refs):
    fars, (corr, energy, edges, squares, frames, partial) = refs[:-6], refs[-6:]
    rows, width = corr.shape
    width //= 2
    swap = odd[0] == 1
    far = jnp.concatenate([ref[...] for ref in fars], 1)
    for side, tile in enumerate((jnp.where(swap, far, own[...]), jnp.where(swap, own[...], far))):
        columns = slice(side * width, (side + 1) * width)
        corr[:, columns] = correlate(weights, tile, frames, partial, rows, width)
        sums = channel_squares(active[...], tile)
        energy[:, columns] = line_sums(sums, span)[:, :width]
        head, tail = slice(side * span, (side + 1) * span), slice((2 + side) * span, (3 + side) * span)
        edges[:, head], squares[:, head] = tile[:, :span], sums[:, :span]
        edges[:, tail], squares[:, tail] = tile[:, width:], sums[:, width:]


def outer_call(odd, weights, active, own, fars, span):
    rows, chans = active.shape
    width = own.shape[1] - span
    flops = 2 * weights.shape[0] * weights.shape[1] * 2 * width
    shape = jax.ShapeDtypeStruct((rows, 2 * width), jnp.float32)
    return pl.pallas_call(
        functools.partial(outer_kernel, span),
        out_shape=(
            shape,
            shape,
            jax.ShapeDtypeStruct((chans, 4 * span), own.dtype),
            jax.ShapeDtypeStruct((rows, 4 * span), jnp.float32),
        ),
        in_specs=[pl.BlockSpec(memory_space=pltpu.SMEM)] + [IN_VMEM] * (3 + len(fars)),
        out_specs=(IN_VMEM,) * 4,
        scratch_shapes=pair_scratch(chans, rows, width, span),
        cost_estimate=pl.CostEstimate(flops=flops, bytes_accessed=1 << 20, transcendentals=0),
        compiler_params=pltpu.CompilerParams(vmem_limit_bytes=32 << 20),
    )(odd, weights, active, own, *fars)


def inner_kernel(span, weights, active, near, edges, squares, corr, energy, frames, partial):
    rows, width = corr.shape
    before, after = slice(2 * span, 3 * span), slice(span, 2 * span)
    signal = jnp.concatenate([edges[:, before], near[...], edges[:, after]], 1)
    sums = channel_squares(active[...], near[...])
    sums = jnp.concatenate([squares[:, before], sums, squares[:, after]], 1)
    energy[...] = line_sums(sums, span)[:, :width]
    corr[...] = correlate(weights, signal, frames, partial, rows, width)


def inner_call(weights, active, near, edges, squares, span):
    rows, chans = active.shape
    width = span + near.shape[1]
    flops = 2 * weights.shape[0] * weights.shape[1] * width
    shape = jax.ShapeDtypeStruct((rows, width), jnp.float32)
    return pl.pallas_call(
        functools.partial(inner_kernel, span),
        out_shape=(shape, shape),
        in_specs=[IN_VMEM] * 5,
        out_specs=(IN_VMEM,) * 2,
        scratch_shapes=pair_scratch(chans, rows, width, span),
        cost_estimate=pl.CostEstimate(flops=flops, bytes_accessed=1 << 20, transcendentals=0),
        compiler_params=pltpu.CompilerParams(vmem_limit_bytes=32 << 20),
    )(weights, active, near, edges, squares)


def middle_kernel(span, missing, weights, active, part, edges, squares, corr, energy, frames, partial):
    rows, width = corr.shape
    gap = jnp.zeros((part.shape[0], missing), part.dtype)
    before, after = slice(3 * span, 4 * span), slice(0, span)
    signal = jnp.concatenate([edges[:, before], part[...], gap, edges[:, after]], 1)
    sums = channel_squares(active[...], part[...])
    gap = jnp.zeros((rows, missing), jnp.float32)
    sums = jnp.concatenate([squares[:, before], sums, gap, squares[:, after]], 1)
    energy[...] = line_sums(sums, span)[:, :width]
    corr[...] = correlate(weights, signal, frames, partial, rows, width)


def middle_call(weights, active, part, edges, squares, missing, span):
    rows, chans = active.shape
    width = span + part.shape[1] + missing
    flops = 2 * weights.shape[0] * weights.shape[1] * width
    shape = jax.ShapeDtypeStruct((rows, width), jnp.float32)
    return pl.pallas_call(
        functools.partial(middle_kernel, span, missing),
        out_shape=(shape, shape),
        in_specs=[IN_VMEM] * 5,
        out_specs=(IN_VMEM,) * 2,
        scratch_shapes=pair_scratch(chans, rows, width, span),
        cost_estimate=pl.CostEstimate(flops=flops, bytes_accessed=1 << 20, transcendentals=0),
        compiler_params=pltpu.CompilerParams(vmem_limit_bytes=32 << 20),
    )(weights, active, part, edges, squares)


def late_kernel(span, ways, place, order, weights, active, part, outer_corr, outer_energy, inner_corr, inner_energy, middle_corr, middle_energy, *refs):
    outs, (corr_all, energy_all, frames, partial) = refs[:ways], refs[ways:]
    rows, total = corr_all.shape
    side, inner = outer_corr.shape[1] // 2, inner_corr.shape[1]
    start = total - span - part.shape[1]
    kept = start - 2 * side - inner
    sums = channel_squares(active[...], part[...])
    sums = line_sums(jnp.concatenate([jnp.zeros((rows, span), jnp.float32), sums], 1), span)
    alone = correlate_alone(weights, part[...], frames, partial, rows)
    for whole, outer, between, middle, added in (
        (energy_all, outer_energy, inner_energy, middle_energy, sums),
        (corr_all, outer_corr, inner_corr, middle_corr, alone),
    ):
        whole[:, :side] = outer[:, :side]
        whole[:, side : side + inner] = between[...]
        whole[:, side + inner : 2 * side + inner] = outer[:, side:]
        whole[:, start - kept : start] = middle[:, :kept]
        whole[:, start:] = middle[:, kept:] + added
    share(place, order, total // order.shape[0], corr_all, energy_all, outs)


def late_call(place, order, weights, active, part, early, middle, span, ways):
    rows = active.shape[0]
    chans, width = part.shape
    total = sum(early[index].shape[1] for index in (0, 2)) + middle[0].shape[1]
    shape = jax.ShapeDtypeStruct((2 * rows, total // ways), jnp.float32)
    flops = 2 * weights.shape[0] * weights.shape[1] * width
    return pl.pallas_call(
        functools.partial(late_kernel, span, ways),
        out_shape=(shape,) * ways,
        in_specs=[pl.BlockSpec(memory_space=pltpu.SMEM)] * 2 + [IN_VMEM] * (3 + len(early) + len(middle)),
        out_specs=(IN_VMEM,) * ways,
        scratch_shapes=[pltpu.VMEM((rows, total), jnp.float32)] * 2
        + [
            pltpu.VMEM((FRAMES * chans, width + LANE), jnp.bfloat16),
            pltpu.VMEM((weights.shape[0], width + LANE), jnp.float32),
        ],
        cost_estimate=pl.CostEstimate(flops=flops, bytes_accessed=1 << 20, transcendentals=0),
        compiler_params=pltpu.CompilerParams(vmem_limit_bytes=32 << 20),
    )(place, order, weights, active, part, *early, *middle)


def share(place, order, tile, corr_all, energy_all, outs):
    rows, total = corr_all.shape
    ways = len(outs)
    count = total // tile // ways
    for shift in range(ways):
        group = lax.rem(place[0] + shift, ways) * count
        for item in range(count):
            start = pl.multiple_of(order[group + item] * tile, LANE)
            columns = slice(item * tile, (item + 1) * tile)
            outs[shift][0:rows, columns] = corr_all[:, pl.ds(start, tile)]
            outs[shift][rows : 2 * rows, columns] = energy_all[:, pl.ds(start, tile)]


def line_sums(values, span):
    reach = 1
    while reach < span:
        values = values + jnp.concatenate([values[:, reach:], values[:, :reach]], 1)
        reach *= 2
    return values


def pack_kernel(span, tile, pairs, place, order, *refs):
    corrs, squares = refs[:pairs], refs[pairs : 2 * pairs]
    outs, corr_all, energy_all = refs[2 * pairs : -2], refs[-2], refs[-1]
    corr = jnp.concatenate([ref[...] for ref in corrs], 1)
    corr_all[...] = jnp.concatenate([corr[:, tile:], corr[:, :tile]], 1)
    energy = line_sums(jnp.concatenate([ref[...] for ref in squares], 1), span)
    energy_all[...] = jnp.concatenate([energy[:, tile:], energy[:, :tile]], 1)
    share(place, order, tile, corr_all, energy_all, outs)


def pack_call(place, order, corrs, squares, span, ways):
    rows, width = corrs[0].shape
    pairs = len(corrs)
    total = pairs * width
    shape = jax.ShapeDtypeStruct((2 * rows, total // ways), jnp.float32)
    return pl.pallas_call(
        functools.partial(pack_kernel, span, width // 2, pairs),
        out_shape=(shape,) * ways,
        in_specs=[pl.BlockSpec(memory_space=pltpu.SMEM)] * 2 + [IN_VMEM] * (2 * pairs),
        out_specs=(IN_VMEM,) * ways,
        scratch_shapes=[pltpu.VMEM((rows, total), jnp.float32)] * 2,
        compiler_params=pltpu.CompilerParams(vmem_limit_bytes=16 << 20),
    )(place, order, *corrs, *squares)


def split_kernel(ways, count, place, *refs):
    ins, outs, held = refs[:count], refs[count:-1], refs[-1]
    total = ins[0][...]
    for ref in ins[1:]:
        total = total + ref[...]
    held[...] = total
    part = held.shape[1] // ways
    for shift in range(ways):
        start = pl.multiple_of(lax.rem(place[0] + shift, ways) * part, LANE)
        outs[shift][...] = held[:, pl.ds(start, part)]


def split_call(place, parts, ways):
    rows, width = parts[0].shape
    shape = jax.ShapeDtypeStruct((rows, width // ways), jnp.float32)
    return pl.pallas_call(
        functools.partial(split_kernel, ways, len(parts)),
        out_shape=(shape,) * ways,
        in_specs=[pl.BlockSpec(memory_space=pltpu.SMEM)] + [IN_VMEM] * len(parts),
        out_specs=(IN_VMEM,) * ways,
        scratch_shapes=[pltpu.VMEM((rows, width), jnp.float32)],
        compiler_params=pltpu.CompilerParams(vmem_limit_bytes=16 << 20),
    )(place, *parts)


def score_kernel(span, count, stats, *refs):
    ins, out = refs[:count], refs[count]
    total = ins[0][...]
    for ref in ins[1:]:
        total = total + ref[...]
    rows = out.shape[0]
    template_energy = stats[0:rows, 0:1]
    active_count = stats[rows:, 0:1]
    factor = jnp.sqrt(span * active_count)
    energy = total[rows:, :]
    out[...] = total[0:rows, :] * factor / jnp.sqrt(energy * template_energy + EPSILON)


def score_call(stats, parts, span):
    rows, width = parts[0].shape
    return pl.pallas_call(
        functools.partial(score_kernel, span, len(parts)),
        out_shape=jax.ShapeDtypeStruct((rows // 2, width), jnp.float32),
        in_specs=[IN_VMEM] * (1 + len(parts)),
        out_specs=IN_VMEM,
        compiler_params=pltpu.CompilerParams(vmem_limit_bytes=16 << 20),
    )(stats, *parts)


def exchange(parts, axis):
    return [parts[0]] + [shifted(part, axis, shift) for shift, part in enumerate(parts) if shift]


def paired(x, axis, bit):
    return lax.ppermute(x, axis, [(i, i ^ bit) for i in range(lax.axis_size(axis))])


def relays(circle, ways):
    return circle == ways == 4


def relayed_sums(traces, weights, active, sub_place, order, span, ways):
    half = traces.shape[1] // 2
    fars = [paired(traces[:, :half], "tm", 2)]
    fars.append(paired(traces[:, half:], "tm", 2))
    near = paired(traces, "tm", 1)
    before = paired(fars[0], "tm", 1)
    part = paired(fars[1], "tm", 1)
    odd = (lax.axis_index("tm") % 2).astype(jnp.int32)[None]
    *outer, edges, squares = outer_call(odd, weights, active, traces, fars, span)
    early = (*outer, *inner_call(weights, active, near, edges, squares, span))
    middle = middle_call(weights, active, before, edges, squares, part.shape[1], span)
    return late_call(sub_place, order, weights, active, part, early, middle, span, ways)


def routes(circle, chan_ways, sub_ways):
    held = circle // (chan_ways * sub_ways)
    table = []
    for place in range(circle):
        chan = place // held // sub_ways
        slots = [(s, c, h) for s in range(sub_ways) for c in range(chan_ways) for h in range(held)]
        tiles = sorted(range(circle), key=lambda t: -abs(t - place))
        ranked = sorted(range(circle), key=lambda k: (slots[k][1] != chan, -slots[k][0]))
        row = [0] * circle
        for slot, time_tile in zip(ranked, tiles):
            row[slot] = time_tile
        table.append(row)
    return table


def gathered_sums(traces, weights, active, sub_place, order, span, ways):
    circle = lax.axis_size("tm")
    arrived = {0: traces}
    for hop in range(1, circle // 2 + 1):
        for near in dict.fromkeys((hop, circle - hop)):
            arrived[near] = shifted(traces, "tm", -near)
    corrs, squares = [], []
    for pair in range(circle // 2):
        first, second = arrived[(2 * pair - 1) % circle], arrived[2 * pair]
        head = arrived[(2 * pair + 1) % circle]
        corr, square = pair_call(weights, active, first, second, head, span)
        corrs.append(corr)
        squares.append(square)
    return pack_call(sub_place, order, corrs, squares, span, ways)


def on_device(traces, templates, channel_mask):
    tile = traces.shape[1]
    rows, _, span = templates.shape
    circle = lax.axis_size("tm")
    chan_ways, sub_ways = lax.axis_size("chan"), lax.axis_size("sub")
    active = channel_mask.astype(jnp.bfloat16)
    masked = templates * active[:, :, None]
    weights = arrange(masked, span)
    wide = masked.astype(jnp.float32)
    template_energy = jnp.sum(wide * wide, axis=(1, 2))
    active_count = jnp.sum(channel_mask, axis=1).astype(jnp.float32)
    stats = jnp.broadcast_to(jnp.concatenate([template_energy, active_count])[:, None], (2 * rows, LANE))
    for axis in ("sub", "chan"):
        others = [shifted(stats, axis, by) for by in range(1, lax.axis_size(axis))]
        stats = sum(others, stats)
    sub_place = lax.axis_index("sub").astype(jnp.int32)[None]
    chan_place = lax.axis_index("chan").astype(jnp.int32)[None]

    ways = chan_ways * sub_ways
    held = circle // ways
    relayed = relays(circle, ways)
    if relayed:
        table = routes(circle, chan_ways, sub_ways)
        order = (jnp.array(table, jnp.int32)[lax.axis_index("tm")] + lax.axis_index("tm")) % circle
    else:
        table = [[(slot + place) % circle for slot in range(circle)] for place in range(circle)]
        order = jnp.arange(circle, dtype=jnp.int32)
    sums = relayed_sums if relayed else gathered_sums
    parts = sums(traces, weights, active, sub_place, order.astype(jnp.int32), span, sub_ways)
    parts = exchange(parts, "sub")
    parts = exchange(split_call(chan_place, parts, chan_ways), "chan")
    scores = score_call(stats, parts, span)

    received = []
    for piece in range(held):
        pairs = []
        for place in range(circle):
            for chan in range(chan_ways):
                for sub in range(sub_ways):
                    source = (place * chan_ways + chan) * sub_ways + sub
                    slot = (sub * chan_ways + chan) * held + piece
                    pairs.append((source, table[place][slot] * ways + place // held))
        block = scores[:, piece * tile : (piece + 1) * tile]
        received.append(lax.ppermute(block, ("tm", "chan", "sub"), pairs))
    if held == 1:
        return received[0]
    turn = (lax.axis_index("tm") - jnp.arange(held)) % held
    return jnp.stack(received)[turn].reshape(held * rows, tile)


def solution(mesh):
    placed = (
        P(("chan", "sub"), ("groups", "tm")),
        P("tm", ("chan", "sub"), None),
        P("tm", ("chan", "sub")),
    )
    return jax.shard_map(
        on_device,
        mesh=mesh,
        in_specs=placed,
        out_specs=P(("chan", "sub"), ("groups", "tm")),
        check_vma=False,
    )
```

time: 35.7 us -> 39.6 us (1.11)
  waiting for transfers between devices: 11.4 us -> 16.5 us
  starting transfers between devices: 14.3 us -> 11.9 us
  Pallas kernels: 5.56 us -> 6.43 us
    ppermute x5, waiting for transfers between devices: 5.29 us -> 10.5 us  [paired(): lax.ppermute(x, axis, [(i, i ^ bit) for i in range(lax.axis_size(axis))])]
    ppermute x5, starting transfers between devices: 10.5 us -> 8.13 us  [paired(): lax.ppermute(x, axis, [(i, i ^ bit) for i in range(lax.axis_size(axis))])]
    ppermute x2 -> x4, starting transfers between devices: 1.63 us -> 2.89 us  [shifted(): return lax.ppermute(x, axis, [(i, (i + by) % count) for i in range(count)])]
    ppermute x2 -> x4, waiting for transfers between devices: 4.2 us -> 2.96 us  [shifted(): return lax.ppermute(x, axis, [(i, (i + by) % count) for i in range(count)])]
    ppermute x1, waiting for transfers between devices: 1.89 us -> 3.06 us  [on_device(): received.append(lax.ppermute(block, ('tm', 'chan', 'sub'), pairs))]
    ppermute x1, starting transfers between devices: 2.08 us -> 0.92 us  [on_device(): received.append(lax.ppermute(block, ('tm', 'chan', 'sub'), pairs))]
    pallas_call x2 -> x3, Pallas kernels: 3.79 us -> 4.88 us  [the longest x1 2.21 us: outer_call(): pl.pallas_call(functools.partial(outer_kernel, span), out_shape=(shape, s...]
    convert_element_type x0 -> x1, other arithmetic: none -> 0.88 us  [on_device(): active = channel_mask.astype(jnp.bfloat16)]
  transfers between devices with their start and end apart: 8 -> 10, of which waited for: 6 -> 5; matrix products, arithmetic and copies ran while one was open for 10% -> 10% of each run, Pallas kernels for 11% -> 16%
where the time goes in v1:
time: 39.6 us; the launch traced here: 39.4 us
  waiting for transfers between devices  16.5 us (42%)
  starting transfers between devices  11.9 us (30%)
  Pallas kernels  6.43 us (16%)
  local copies, waits for them, and re-layouts  2.31 us (6%)
  other arithmetic  2.07 us (5%)
    ppermute x5, waiting for transfers between devices, paired(): lax.ppermute(x, axis, [(i, i ^ bit) for i in range(lax.axis_size(axis))])  10.5 us
    ppermute x5, starting transfers between devices, paired(): lax.ppermute(x, axis, [(i, i ^ bit) for i in range(lax.axis_size(axis))])  8.13 us
    ppermute x1, waiting for transfers between devices, on_device(): received.append(lax.ppermute(block, ('tm', 'chan', 'sub'), pairs))  3.06 us
    ppermute x4, waiting for transfers between devices, shifted(): return lax.ppermute(x, axis, [(i, (i + by) % count) for i in range(count)])  2.96 us
    ppermute x4, starting transfers between devices, shifted(): return lax.ppermute(x, axis, [(i, (i + by) % count) for i in range(count)])  2.89 us
    pallas_call x1, Pallas kernels, outer_call(): pl.pallas_call(functools.partial(outer_kernel, span), out_shape=(shape, s...  2.21 us
    pallas_call x1, Pallas kernels, late_call(): pl.pallas_call(functools.partial(late_kernel, span, ways), out_shape=(sha...  1.43 us
    pallas_call x1, Pallas kernels, inner_call(): pl.pallas_call(functools.partial(inner_kernel, span), out_shape=(shape, s...  1.36 us
  transfers between devices with their start and end apart: 10, of which 5 were waited for; matrix products, arithmetic and copies ran while one was open for 10% of the time, Pallas kernels for 16%

profile of v1, /device:TPU:0, one launch (start us, length us, event | category | flops | bytes accessed | tf_op | source)
XLA Modules:
  0.0 39.4 jit_solution(16596245406237426945)
XLA Ops:
  0.0 3.1 %collective-permute-start.5 = (bf16[128,1024]{1,0:T(8,128)(2,1)}, bf16[128,1024]{1,0:T(8,128)(2,1)S(1)}, u32[]{:S(2)}, u32[]{:S(2)}) collective-permute-start(bf16[128,1024]{1,0:T(8,128)(2,1)} %own.1), channel_id=1, source_target_pairs={{0,4},{4,0},{8,12},{12,8},{1,5},{5,1},{9,13},{13,9},{2,6},{6,2},{1... | collective-permute-start | bytes 786440 | tf_op jit(solution)/shard_map/ppermute | solution.py:360
  3.1 1.0 %fusion.1 = (bf16[128,512]{1,0:T(8,128)(2,1)S(1)}, bf16[128,512]{1,0:T(8,128)(2,1)S(1)}) fusion(bf16[128,1024]{1,0:T(8,128)(2,1)} %own.1), kind=kLoop, calls=%fused_computation.8 | loop fusion | bytes 524288 | tf_op jit(solution)/shard_map/slice | solution.py:369
  4.1 2.7 %collective-permute-start.2 = (bf16[128,512]{1,0:T(8,128)(2,1)S(1)}, bf16[128,512]{1,0:T(8,128)(2,1)S(1)}, u32[]{:S(2)}, u32[]{:S(2)}) collective-permute-start(bf16[128,512]{1,0:T(8,128)(2,1)S(1)} %get-tuple-element.32), channel_id=1, source_target_pairs={{0,8},{4,12},{8,0},{12,4},{1,9},{5,13},{9,1},{13,5},{2,10},{6,14},... | collective-permute-start | bytes 393224 | tf_op jit(solution)/shard_map/ppermute | solution.py:360
  6.7 0.3 collective-permute-start.4
  7.0 0.9 %fusion.2 = (bf16[8,128]{1,0:T(8,128)(2,1)S(1)}, s32[8]{0:T(128)S(1)}) fusion(s32[8,128]{1,0:T(8,128)} %param.6), kind=kLoop, calls=%fused_computation.9 | loop fusion | flops 2040 | bytes 6176 | tf_op jit(solution)/shard_map/convert_element_type | solution.py:417
  7.9 0.3 copy.6
  8.2 0.3 multiply_reduce_fusion
  8.5 0.1 pad_maximum_fusion
  8.6 0.1 broadcast_in_dim.16
  8.6 0.0 collective-permute-start
  8.6 9.8 %collective-permute-done.4.refs_0_ = bf16[128,512]{1,0:T(8,128)(2,1)S(1)} collective-permute-done((bf16[128,512]{1,0:T(8,128)(2,1)S(1)}, bf16[128,512]{1,0:T(8,128)(2,1)S(1)}, u32[]{:S(2)}, u32[]{:S(2)}) %collective-permute-start.4) | collective-permute-done | bytes 131104 | tf_op jit(solution)/shard_map/ppermute | solution.py:360
  18.4 0.7 %and_select_fusion.order = s32[4]{0:T(128)S(1)} fusion(s32[4,4]{1,0:T(4,128)} %constant.43.clone, s32[]{:T(128)S(6)} %select_n.16, s32[]{:T(128)S(6)} %axis_index.46), kind=kLoop, calls=%fused_computation.5 | loop fusion | flops 48 | bytes 40 | tf_op jit(solution)/shard_map/jit(remainder)/select_n | solution.py:435
  19.1 0.3 copy.7
  19.5 0.0 collective-permute-done.2.refs_1_
  19.5 2.1 %collective-permute-start.3 = (bf16[128,512]{1,0:T(8,128)(2,1)S(1)}, bf16[128,512]{1,0:T(8,128)(2,1)S(1)}, u32[]{:S(2)}, u32[]{:S(2)}) collective-permute-start(bf16[128,512]{1,0:T(8,128)(2,1)S(1)} %collective-permute-done.2.refs_1_), channel_id=1, source_target_pairs={{0,4},{4,0},{8,12},{12,8},{1,5},{5,1},{9,13},{13,9},{2,6},{6,2},{1... | collective-permute-start | bytes 393224 | tf_op jit(solution)/shard_map/ppermute | solution.py:360
  21.6 2.2 %shard_map.46 = (f32[8,1536]{1,0:T(8,128)S(1)}, f32[8,1536]{1,0:T(8,128)S(1)}, bf16[128,1024]{1,0:T(8,128)(2,1)S(1)}, f32[8,1024]{1,0:T(8,128)S(1)}) custom-call(s32[1]{0:T(128)} %bitcast.6.odd, bf16[512,512]{1,0:T(8,128)(2,1)S(1)} %bitcast.9, bf16[8,128]{1,0:T(8,128)(2,1)S(1)} %get-tuple-element.33.active, bf16[128,1024]{1,0:T(8,128)(2,1)S(1)} %copy-done, ...), custom_call_target="tpu_custom_call" | custom-call | flops 805306368 | bytes 1048576 | tf_op jit(solution)/shard_map/pallas_call | solution.py:148
  23.8 0.7 %collective-permute-done.6.part = bf16[128,512]{1,0:T(8,128)(2,1)S(1)} collective-permute-done((bf16[128,512]{1,0:T(8,128)(2,1)S(1)}, bf16[128,512]{1,0:T(8,128)(2,1)S(1)}, u32[]{:S(2)}, u32[]{:S(2)}) %collective-permute-start.6) | collective-permute-done | bytes 131104 | tf_op jit(solution)/shard_map/ppermute | solution.py:360
  24.5 1.3 %shard_map.48 = (f32[8,1280]{1,0:T(8,128)S(1)}, f32[8,1280]{1,0:T(8,128)S(1)}) custom-call(bf16[512,512]{1,0:T(8,128)(2,1)S(1)} %bitcast.10, bf16[8,128]{1,0:T(8,128)(2,1)S(1)} %get-tuple-element.33.active, bf16[128,512]{1,0:T(8,128)(2,1)S(1)} %collective-permute-done.6.part, bf16[128,1024]{1,0:T(8,128)(2,1)S(1)} %get-tuple-element.19.edges, ...), custom_call_target="tpu_custom_call" | custom-call | flops 671088640 | bytes 1048576 | tf_op jit(solution)/shard_map/pallas_call | solution.py:207
  25.8 0.0 collective-permute-done.5.near
  25.8 1.4 %shard_map.47 = (f32[8,1280]{1,0:T(8,128)S(1)}, f32[8,1280]{1,0:T(8,128)S(1)}) custom-call(bf16[512,512]{1,0:T(8,128)(2,1)S(1)} %bitcast.11, bf16[8,128]{1,0:T(8,128)(2,1)S(1)} %get-tuple-element.33.active, bf16[128,1024]{1,0:T(8,128)(2,1)S(1)} %collective-permute-done.5.near, bf16[128,1024]{1,0:T(8,128)(2,1)S(1)} %get-tuple-element.19.edges, ...), custom_call_target="tpu_custom_call" | custom-call | flops 671088640 | bytes 1048576 | tf_op jit(solution)/shard_map/pallas_call | solution.py:179
  27.2 1.4 %shard_map.49 = (f32[16,2048]{1,0:T(8,128)S(1)}, f32[16,2048]{1,0:T(8,128)S(1)}) custom-call(s32[1]{0:T(128)} %bitcast.1.place, s32[4]{0:T(128)S(1)} %and_select_fusion.order, bf16[512,512]{1,0:T(8,128)(2,1)S(1)} %bitcast.12, bf16[8,128]{1,0:T(8,128)(2,1)S(1)} %get-tuple-element.33.active, bf16[128,512]{1,0:T(8,128)(2,1)S(1)} %collective-permute-done.3.part, ...), custom_call_target="tpu_custom_call" | custom-call | flops 268435456 | bytes 1048576 | tf_op jit(solution)/shard_map/pallas_call | solution.py:245
  28.6 0.1 collective-permute-start.7
  28.7 0.1 broadcast_add_fusion
  28.8 1.5 %collective-permute-start.1 = (f32[16,128]{1,0:T(8,128)S(1)}, f32[16,128]{1,0:T(8,128)S(1)}, u32[]{:S(2)}, u32[]{:S(2)}) collective-permute-start(f32[16,128]{1,0:T(8,128)S(1)} %broadcast_add_fusion), channel_id=1, source_target_pairs={{0,2},{2,0},{1,3},{3,1},{4,6},{6,4},{5,7},{7,5},{8,10},{10,8},{9,1... | collective-permute-start | bytes 24584 | tf_op jit(solution)/shard_map/ppermute | solution.py:20
  30.3 1.3 %collective-permute-start.8 = (f32[16,1024]{1,0:T(8,128)S(1)}, f32[16,1024]{1,0:T(8,128)S(1)}, u32[]{:S(2)}, u32[]{:S(2)}) collective-permute-start(f32[16,1024]{1,0:T(8,128)S(1)} %get-tuple-element.28), channel_id=1, source_target_pairs={{0,2},{2,0},{1,3},{3,1},{4,6},{6,4},{5,7},{7,5},{8,10},{10,8},{9,1... | collective-permute-start | bytes 196616 | tf_op jit(solution)/shard_map/ppermute | solution.py:20
  31.6 0.8 %collective-permute-done.1 = f32[16,128]{1,0:T(8,128)S(1)} collective-permute-done((f32[16,128]{1,0:T(8,128)S(1)}, f32[16,128]{1,0:T(8,128)S(1)}, u32[]{:S(2)}, u32[]{:S(2)}) %collective-permute-start.1) | collective-permute-done | bytes 8224 | tf_op jit(solution)/shard_map/ppermute | solution.py:20
  32.5 0.1 fusion.3.stats
  32.5 2.1 %collective-permute-done.8.refs_1_ = f32[16,1024]{1,0:T(8,128)S(1)} collective-permute-done((f32[16,1024]{1,0:T(8,128)S(1)}, f32[16,1024]{1,0:T(8,128)S(1)}, u32[]{:S(2)}, u32[]{:S(2)}) %collective-permute-start.8) | collective-permute-done | bytes 65568 | tf_op jit(solution)/shard_map/ppermute | solution.py:20
  34.7 0.1 shard_map.51
  34.8 0.9 %collective-permute-start.9 = (f32[8,1024]{1,0:T(8,128)S(1)}, f32[8,1024]{1,0:T(8,128)S(1)}, u32[]{:S(2)}, u32[]{:S(2)}) collective-permute-start(f32[8,1024]{1,0:T(8,128)S(1)} %shard_map.51), channel_id=1, source_target_pairs={{0,8},{1,12},{2,0},{3,4},{4,1},{5,13},{6,5},{7,9},{8,10},{9,14},{1... | collective-permute-start | bytes 98312 | tf_op jit(solution)/shard_map/ppermute | solution.py:455
  35.7 3.1 %collective-permute-done.9 = f32[8,1024]{1,0:T(8,128)S(1)} collective-permute-done((f32[8,1024]{1,0:T(8,128)S(1)}, f32[8,1024]{1,0:T(8,128)S(1)}, u32[]{:S(2)}, u32[]{:S(2)}) %collective-permute-start.9) | collective-permute-done | bytes 32800 | tf_op jit(solution)/shard_map/ppermute | solution.py:455
  38.7 0.6 %copy.9 = f32[8,1024]{1,0:T(8,128)} copy(f32[8,1024]{1,0:T(8,128)S(1)} %collective-permute-done.9) | data formatting | bytes 65536
  (10 shorter events, 0.0 us)
Async XLA Ops:
  0.0 7.9 %copy-start.1 = (bf16[8,128,256]{2,1,0:T(8,128)(2,1)S(1)}, bf16[8,128,256]{2,1,0:T(8,128)(2,1)}, u32[]{:S(2)}) copy-start(bf16[8,128,256]{2,1,0:T(8,128)(2,1)} %param.5) | copy-start | bytes 1572868
  0.0 25.8 %collective-permute-start.5 = (bf16[128,1024]{1,0:T(8,128)(2,1)}, bf16[128,1024]{1,0:T(8,128)(2,1)S(1)}, u32[]{:S(2)}, u32[]{:S(2)}) collective-permute-start(bf16[128,1024]{1,0:T(8,128)(2,1)} %own.1), channel_id=1, source_target_pairs={{0,4},{4,0},{8,12},{12,8},{1,5},{5,1},{9,13},{13,9},{2,6},{6,2},{1... | collective-permute-start | bytes 786440 | tf_op jit(solution)/shard_map/ppermute | solution.py:360
  4.1 15.5 %collective-permute-start.2 = (bf16[128,512]{1,0:T(8,128)(2,1)S(1)}, bf16[128,512]{1,0:T(8,128)(2,1)S(1)}, u32[]{:S(2)}, u32[]{:S(2)}) collective-permute-start(bf16[128,512]{1,0:T(8,128)(2,1)S(1)} %get-tuple-element.32), channel_id=1, source_target_pairs={{0,8},{4,12},{8,0},{12,4},{1,9},{5,13},{9,1},{13,5},{2,10},{6,14},... | collective-permute-start | bytes 393224 | tf_op jit(solution)/shard_map/ppermute | solution.py:360
  6.7 11.7 %collective-permute-start.4 = (bf16[128,512]{1,0:T(8,128)(2,1)S(1)}, bf16[128,512]{1,0:T(8,128)(2,1)S(1)}, u32[]{:S(2)}, u32[]{:S(2)}) collective-permute-start(bf16[128,512]{1,0:T(8,128)(2,1)S(1)} %get-tuple-element.31), channel_id=1, source_target_pairs={{0,8},{4,12},{8,0},{12,4},{1,9},{5,13},{9,1},{13,5},{2,10},{6,14},... | collective-permute-start | bytes 393224 | tf_op jit(solution)/shard_map/ppermute | solution.py:360
  8.6 20.1 %collective-permute-start = (f32[16,128]{1,0:T(8,128)S(1)}, f32[16,128]{1,0:T(8,128)S(1)}, u32[]{:S(2)}, u32[]{:S(2)}) collective-permute-start(f32[16,128]{1,0:T(8,128)S(1)} %broadcast_in_dim.16), channel_id=1, source_target_pairs={{0,1},{1,0},{2,3},{3,2},{4,5},{5,4},{6,7},{7,6},{8,9},{9,8},{10,11... | collective-permute-start | bytes 24584 | tf_op jit(solution)/shard_map/ppermute | solution.py:20
  18.4 6.0 %collective-permute-start.6 = (bf16[128,512]{1,0:T(8,128)(2,1)S(1)}, bf16[128,512]{1,0:T(8,128)(2,1)S(1)}, u32[]{:S(2)}, u32[]{:S(2)}) collective-permute-start(bf16[128,512]{1,0:T(8,128)(2,1)S(1)} %collective-permute-done.4.refs_0_), channel_id=1, source_target_pairs={{0,4},{4,0},{8,12},{12,8},{1,5},{5,1},{9,13},{13,9},{2,6},{6,2},{1... | collective-permute-start | bytes 393224 | tf_op jit(solution)/shard_map/ppermute | solution.py:360
  19.1 2.5 %copy-start = (bf16[128,1024]{1,0:T(8,128)(2,1)S(1)}, bf16[128,1024]{1,0:T(8,128)(2,1)}, u32[]{:S(2)}) copy-start(bf16[128,1024]{1,0:T(8,128)(2,1)} %own.1) | copy-start | bytes 786436
  19.5 7.7 %collective-permute-start.3 = (bf16[128,512]{1,0:T(8,128)(2,1)S(1)}, bf16[128,512]{1,0:T(8,128)(2,1)S(1)}, u32[]{:S(2)}, u32[]{:S(2)}) collective-permute-start(bf16[128,512]{1,0:T(8,128)(2,1)S(1)} %collective-permute-done.2.refs_1_), channel_id=1, source_target_pairs={{0,4},{4,0},{8,12},{12,8},{1,5},{5,1},{9,13},{13,9},{2,6},{6,2},{1... | collective-permute-start | bytes 393224 | tf_op jit(solution)/shard_map/ppermute | solution.py:360
  28.6 1.7 %collective-permute-start.7 = (f32[16,2048]{1,0:T(8,128)S(1)}, f32[16,2048]{1,0:T(8,128)S(1)}, u32[]{:S(2)}, u32[]{:S(2)}) collective-permute-start(f32[16,2048]{1,0:T(8,128)S(1)} %get-tuple-element.26), channel_id=1, source_target_pairs={{0,1},{1,0},{2,3},{3,2},{4,5},{5,4},{6,7},{7,6},{8,9},{9,8},{10,11... | collective-permute-start | bytes 393224 | tf_op jit(solution)/shard_map/ppermute | solution.py:20
  28.8 3.7 %collective-permute-start.1 = (f32[16,128]{1,0:T(8,128)S(1)}, f32[16,128]{1,0:T(8,128)S(1)}, u32[]{:S(2)}, u32[]{:S(2)}) collective-permute-start(f32[16,128]{1,0:T(8,128)S(1)} %broadcast_add_fusion), channel_id=1, source_target_pairs={{0,2},{2,0},{1,3},{3,1},{4,6},{6,4},{5,7},{7,5},{8,10},{10,8},{9,1... | collective-permute-start | bytes 24584 | tf_op jit(solution)/shard_map/ppermute | solution.py:20
  30.3 4.3 %collective-permute-start.8 = (f32[16,1024]{1,0:T(8,128)S(1)}, f32[16,1024]{1,0:T(8,128)S(1)}, u32[]{:S(2)}, u32[]{:S(2)}) collective-permute-start(f32[16,1024]{1,0:T(8,128)S(1)} %get-tuple-element.28), channel_id=1, source_target_pairs={{0,2},{2,0},{1,3},{3,1},{4,6},{6,4},{5,7},{7,5},{8,10},{10,8},{9,1... | collective-permute-start | bytes 196616 | tf_op jit(solution)/shard_map/ppermute | solution.py:20
  34.8 4.0 %collective-permute-start.9 = (f32[8,1024]{1,0:T(8,128)S(1)}, f32[8,1024]{1,0:T(8,128)S(1)}, u32[]{:S(2)}, u32[]{:S(2)}) collective-permute-start(f32[8,1024]{1,0:T(8,128)S(1)} %shard_map.51), channel_id=1, source_target_pairs={{0,8},{1,12},{2,0},{3,4},{4,1},{5,13},{6,5},{7,9},{8,10},{9,14},{1... | collective-permute-start | bytes 98312 | tf_op jit(solution)/shard_map/ppermute | solution.py:455

commit v2 on v1

--- a/solution.py
+++ b/solution.py
@@ -215,7 +215,7 @@
     )(weights, active, part, edges, squares)
 
 
-def late_kernel(span, ways, place, order, weights, active, part, outer_corr, outer_energy, inner_corr, inner_energy, middle_corr, middle_energy, *refs):
+def late_kernel(span, ways, table, place, weights, active, part, outer_corr, outer_energy, inner_corr, inner_energy, middle_corr, middle_energy, *refs):
     outs, (corr_all, energy_all, frames, partial) = refs[:ways], refs[ways:]
     rows, total = corr_all.shape
     side, inner = outer_corr.shape[1] // 2, inner_corr.shape[1]
@@ -233,19 +233,19 @@
         whole[:, side + inner : 2 * side + inner] = outer[:, side:]
         whole[:, start - kept : start] = middle[:, :kept]
         whole[:, start:] = middle[:, kept:] + added
-    share(place, order, total // order.shape[0], corr_all, energy_all, outs)
-
-
-def late_call(place, order, weights, active, part, early, middle, span, ways):
+    share(place, table, total // len(table), corr_all, energy_all, outs)
+
+
+def late_call(place, table, weights, active, part, early, middle, span, ways):
     rows = active.shape[0]
     chans, width = part.shape
     total = sum(early[index].shape[1] for index in (0, 2)) + middle[0].shape[1]
     shape = jax.ShapeDtypeStruct((2 * rows, total // ways), jnp.float32)
     flops = 2 * weights.shape[0] * weights.shape[1] * width
     return pl.pallas_call(
-        functools.partial(late_kernel, span, ways),
+        functools.partial(late_kernel, span, ways, table),
         out_shape=(shape,) * ways,
-        in_specs=[pl.BlockSpec(memory_space=pltpu.SMEM)] * 2 + [IN_VMEM] * (3 + len(early) + len(middle)),
+        in_specs=[pl.BlockSpec(memory_space=pltpu.SMEM)] + [IN_VMEM] * (3 + len(early) + len(middle)),
         out_specs=(IN_VMEM,) * ways,
         scratch_shapes=[pltpu.VMEM((rows, total), jnp.float32)] * 2
         + [
@@ -254,17 +254,24 @@
         ],
         cost_estimate=pl.CostEstimate(flops=flops, bytes_accessed=1 << 20, transcendentals=0),
         compiler_params=pltpu.CompilerParams(vmem_limit_bytes=32 << 20),
-    )(place, order, weights, active, part, *early, *middle)
-
-
-def share(place, order, tile, corr_all, energy_all, outs):
+    )(place, weights, active, part, *early, *middle)
+
+
+def share(place, table, tile, corr_all, energy_all, outs):
     rows, total = corr_all.shape
     ways = len(outs)
     count = total // tile // ways
     for shift in range(ways):
         group = lax.rem(place[0] + shift, ways) * count
         for item in range(count):
-            start = pl.multiple_of(order[group + item] * tile, LANE)
+            position = group + item
+            if table:
+                position = jnp.int32(0)
+                for home, row in enumerate(table):
+                    for slot, value in enumerate(row):
+                        chosen = (place[1] == home) & (group + item == slot)
+                        position = jnp.where(chosen, value, position)
+            start = pl.multiple_of(position * tile, LANE)
             columns = slice(item * tile, (item + 1) * tile)
             outs[shift][0:rows, columns] = corr_all[:, pl.ds(start, tile)]
             outs[shift][rows : 2 * rows, columns] = energy_all[:, pl.ds(start, tile)]
@@ -278,17 +285,17 @@
     return values
 
 
-def pack_kernel(span, tile, pairs, place, order, *refs):
+def pack_kernel(span, tile, pairs, place, *refs):
     corrs, squares = refs[:pairs], refs[pairs : 2 * pairs]
     outs, corr_all, energy_all = refs[2 * pairs : -2], refs[-2], refs[-1]
     corr = jnp.concatenate([ref[...] for ref in corrs], 1)
     corr_all[...] = jnp.concatenate([corr[:, tile:], corr[:, :tile]], 1)
     energy = line_sums(jnp.concatenate([ref[...] for ref in squares], 1), span)
     energy_all[...] = jnp.concatenate([energy[:, tile:], energy[:, :tile]], 1)
-    share(place, order, tile, corr_all, energy_all, outs)
-
-
-def pack_call(place, order, corrs, squares, span, ways):
+    share(place, None, tile, corr_all, energy_all, outs)
+
+
+def pack_call(place, corrs, squares, span, ways):
     rows, width = corrs[0].shape
     pairs = len(corrs)
     total = pairs * width
@@ -296,11 +303,11 @@
     return pl.pallas_call(
         functools.partial(pack_kernel, span, width // 2, pairs),
         out_shape=(shape,) * ways,
-        in_specs=[pl.BlockSpec(memory_space=pltpu.SMEM)] * 2 + [IN_VMEM] * (2 * pairs),
+        in_specs=[pl.BlockSpec(memory_space=pltpu.SMEM)] + [IN_VMEM] * (2 * pairs),
         out_specs=(IN_VMEM,) * ways,
         scratch_shapes=[pltpu.VMEM((rows, total), jnp.float32)] * 2,
         compiler_params=pltpu.CompilerParams(vmem_limit_bytes=16 << 20),
-    )(place, order, *corrs, *squares)
+    )(place, *corrs, *squares)
 
 
 def split_kernel(ways, count, place, *refs):
@@ -364,7 +371,7 @@
     return circle == ways == 4
 
 
-def relayed_sums(traces, weights, active, sub_place, order, span, ways):
+def relayed_sums(traces, weights, active, place, table, span, ways):
     half = traces.shape[1] // 2
     fars = [paired(traces[:, :half], "tm", 2)]
     fars.append(paired(traces[:, half:], "tm", 2))
@@ -375,7 +382,7 @@
     *outer, edges, squares = outer_call(odd, weights, active, traces, fars, span)
     early = (*outer, *inner_call(weights, active, near, edges, squares, span))
     middle = middle_call(weights, active, before, edges, squares, part.shape[1], span)
-    return late_call(sub_place, order, weights, active, part, early, middle, span, ways)
+    return late_call(place, table, weights, active, part, early, middle, span, ways)
 
 
 def routes(circle, chan_ways, sub_ways):
@@ -393,7 +400,7 @@
     return table
 
 
-def gathered_sums(traces, weights, active, sub_place, order, span, ways):
+def gathered_sums(traces, weights, active, place, table, span, ways):
     circle = lax.axis_size("tm")
     arrived = {0: traces}
     for hop in range(1, circle // 2 + 1):
@@ -406,7 +413,7 @@
         corr, square = pair_call(weights, active, first, second, head, span)
         corrs.append(corr)
         squares.append(square)
-    return pack_call(sub_place, order, corrs, squares, span, ways)
+    return pack_call(place, corrs, squares, span, ways)
 
 
 def on_device(traces, templates, channel_mask):
@@ -424,7 +431,7 @@
     for axis in ("sub", "chan"):
         others = [shifted(stats, axis, by) for by in range(1, lax.axis_size(axis))]
         stats = sum(others, stats)
-    sub_place = lax.axis_index("sub").astype(jnp.int32)[None]
+    place = jnp.stack([lax.axis_index("sub"), lax.axis_index("tm")]).astype(jnp.int32)
     chan_place = lax.axis_index("chan").astype(jnp.int32)[None]
 
     ways = chan_ways * sub_ways
@@ -432,12 +439,11 @@
     relayed = relays(circle, ways)
     if relayed:
         table = routes(circle, chan_ways, sub_ways)
-        order = (jnp.array(table, jnp.int32)[lax.axis_index("tm")] + lax.axis_index("tm")) % circle
     else:
         table = [[(slot + place) % circle for slot in range(circle)] for place in range(circle)]
-        order = jnp.arange(circle, dtype=jnp.int32)
     sums = relayed_sums if relayed else gathered_sums
-    parts = sums(traces, weights, active, sub_place, order.astype(jnp.int32), span, sub_ways)
+    spots = [[(time_tile + home) % circle for time_tile in row] for home, row in enumerate(table)]
+    parts = sums(traces, weights, active, place, spots, span, sub_ways)
     parts = exchange(parts, "sub")
     parts = exchange(split_call(chan_place, parts, chan_ways), "chan")
     scores = score_call(stats, parts, span)

time: 39.6 us -> 39.6 us (level)
  other arithmetic: 2.07 us -> 1.45 us
  starting transfers between devices: 11.9 us -> 12.4 us
    select_n x1 -> x0, other arithmetic: 0.7 us -> none  [on_device(): (jnp.array(table, jnp.int32)[lax.axis_index('tm')] + lax.axis_index('tm')...]
    ppermute x5, waiting for transfers between devices: 10.5 us -> 11.1 us  [paired(): lax.ppermute(x, axis, [(i, i ^ bit) for i in range(lax.axis_size(axis))])]
    ppermute x1, waiting for transfers between devices: 3.06 us -> 2.59 us  [on_device(): received.append(lax.ppermute(block, ('tm', 'chan', 'sub'), pairs))]
    ppermute x1, starting transfers between devices: 0.92 us -> 1.39 us  [on_device(): received.append(lax.ppermute(block, ('tm', 'chan', 'sub'), pairs))]
  transfers between devices with their start and end apart: 10 -> 10, of which waited for: 5 -> 5; matrix products, arithmetic and copies ran while one was open for 10% -> 8% of each run, Pallas kernels for 16% -> 16%
where the time goes in v2:
time: 39.6 us; the launch traced here: 39.3 us
  waiting for transfers between devices  16.7 us (42%)
  starting transfers between devices  12.4 us (31%)
  Pallas kernels  6.42 us (16%)
  local copies, waits for them, and re-layouts  2.31 us (6%)
  other arithmetic  1.45 us (4%)
    ppermute x5, waiting for transfers between devices, paired(): lax.ppermute(x, axis, [(i, i ^ bit) for i in range(lax.axis_size(axis))])  11.1 us
    ppermute x5, starting transfers between devices, paired(): lax.ppermute(x, axis, [(i, i ^ bit) for i in range(lax.axis_size(axis))])  8.13 us
    ppermute x4, waiting for transfers between devices, shifted(): return lax.ppermute(x, axis, [(i, (i + by) % count) for i in range(count)])  2.96 us
    ppermute x4, starting transfers between devices, shifted(): return lax.ppermute(x, axis, [(i, (i + by) % count) for i in range(count)])  2.87 us
    ppermute x1, waiting for transfers between devices, on_device(): received.append(lax.ppermute(block, ('tm', 'chan', 'sub'), pairs))  2.59 us
    pallas_call x1, Pallas kernels, outer_call(): pl.pallas_call(functools.partial(outer_kernel, span), out_shape=(shape, s...  2.19 us
    pallas_call x1, Pallas kernels, late_call(): pl.pallas_call(functools.partial(late_kernel, span, ways, table), out_sha...  1.43 us
    ppermute x1, starting transfers between devices, on_device(): received.append(lax.ppermute(block, ('tm', 'chan', 'sub'), pairs))  1.39 us
  transfers between devices with their start and end apart: 10, of which 5 were waited for; matrix products, arithmetic and copies ran while one was open for 8% of the time, Pallas kernels for 16%

profile of v2, /device:TPU:0, one launch (start us, length us, event | category | flops | bytes accessed | tf_op | source)
XLA Modules:
  0.0 39.3 jit_solution(9453343207753116413)
XLA Ops:
  0.0 3.1 %collective-permute-start.5 = (bf16[128,1024]{1,0:T(8,128)(2,1)}, bf16[128,1024]{1,0:T(8,128)(2,1)S(1)}, u32[]{:S(2)}, u32[]{:S(2)}) collective-permute-start(bf16[128,1024]{1,0:T(8,128)(2,1)} %own.1), channel_id=1, source_target_pairs={{0,4},{4,0},{8,12},{12,8},{1,5},{5,1},{9,13},{13,9},{2,6},{6,2},{1... | collective-permute-start | bytes 786440 | tf_op jit(solution)/shard_map/ppermute | solution.py:367
  3.1 1.0 %fusion = (bf16[128,512]{1,0:T(8,128)(2,1)S(1)}, bf16[128,512]{1,0:T(8,128)(2,1)S(1)}) fusion(bf16[128,1024]{1,0:T(8,128)(2,1)} %own.1), kind=kLoop, calls=%fused_computation.5 | loop fusion | bytes 524288 | tf_op jit(solution)/shard_map/slice | solution.py:376
  4.1 2.7 %collective-permute-start.2 = (bf16[128,512]{1,0:T(8,128)(2,1)S(1)}, bf16[128,512]{1,0:T(8,128)(2,1)S(1)}, u32[]{:S(2)}, u32[]{:S(2)}) collective-permute-start(bf16[128,512]{1,0:T(8,128)(2,1)S(1)} %get-tuple-element.32), channel_id=1, source_target_pairs={{0,8},{4,12},{8,0},{12,4},{1,9},{5,13},{9,1},{13,5},{2,10},{6,14},... | collective-permute-start | bytes 393224 | tf_op jit(solution)/shard_map/ppermute | solution.py:367
  6.7 0.3 collective-permute-start.4
  7.0 0.9 %fusion.1 = (bf16[8,128]{1,0:T(8,128)(2,1)S(1)}, s32[8]{0:T(128)S(1)}) fusion(s32[8,128]{1,0:T(8,128)} %param.5), kind=kLoop, calls=%fused_computation.6 | loop fusion | flops 2040 | bytes 6176 | tf_op jit(solution)/shard_map/convert_element_type | solution.py:424
  7.9 0.3 copy.5
  8.2 0.3 multiply_reduce_fusion
  8.5 0.1 pad_maximum_fusion
  8.6 0.1 broadcast_in_dim.6
  8.6 9.8 %collective-permute-done.4.refs_0_ = bf16[128,512]{1,0:T(8,128)(2,1)S(1)} collective-permute-done((bf16[128,512]{1,0:T(8,128)(2,1)S(1)}, bf16[128,512]{1,0:T(8,128)(2,1)S(1)}, u32[]{:S(2)}, u32[]{:S(2)}) %collective-permute-start.4) | collective-permute-done | bytes 131104 | tf_op jit(solution)/shard_map/ppermute | solution.py:367
  18.4 0.1 pad_add_fusion.place
  18.5 0.3 copy.6
  18.9 0.0 collective-permute-done.2.refs_1_
  18.9 2.1 %collective-permute-start.3 = (bf16[128,512]{1,0:T(8,128)(2,1)S(1)}, bf16[128,512]{1,0:T(8,128)(2,1)S(1)}, u32[]{:S(2)}, u32[]{:S(2)}) collective-permute-start(bf16[128,512]{1,0:T(8,128)(2,1)S(1)} %collective-permute-done.2.refs_1_), channel_id=1, source_target_pairs={{0,4},{4,0},{8,12},{12,8},{1,5},{5,1},{9,13},{13,9},{2,6},{6,2},{1... | collective-permute-start | bytes 393224 | tf_op jit(solution)/shard_map/ppermute | solution.py:367
  21.0 2.2 %shard_map.37 = (f32[8,1536]{1,0:T(8,128)S(1)}, f32[8,1536]{1,0:T(8,128)S(1)}, bf16[128,1024]{1,0:T(8,128)(2,1)S(1)}, f32[8,1024]{1,0:T(8,128)S(1)}) custom-call(s32[1]{0:T(128)} %bitcast.6.odd, bf16[512,512]{1,0:T(8,128)(2,1)S(1)} %bitcast.8, bf16[8,128]{1,0:T(8,128)(2,1)S(1)} %get-tuple-element.33.active, bf16[128,1024]{1,0:T(8,128)(2,1)S(1)} %copy-done, ...), custom_call_target="tpu_custom_call" | custom-call | flops 805306368 | bytes 1048576 | tf_op jit(solution)/shard_map/pallas_call | solution.py:148
  23.2 1.3 %collective-permute-done.6.part = bf16[128,512]{1,0:T(8,128)(2,1)S(1)} collective-permute-done((bf16[128,512]{1,0:T(8,128)(2,1)S(1)}, bf16[128,512]{1,0:T(8,128)(2,1)S(1)}, u32[]{:S(2)}, u32[]{:S(2)}) %collective-permute-start.6) | collective-permute-done | bytes 131104 | tf_op jit(solution)/shard_map/ppermute | solution.py:367
  24.5 1.3 %shard_map.39 = (f32[8,1280]{1,0:T(8,128)S(1)}, f32[8,1280]{1,0:T(8,128)S(1)}) custom-call(bf16[512,512]{1,0:T(8,128)(2,1)S(1)} %bitcast.9, bf16[8,128]{1,0:T(8,128)(2,1)S(1)} %get-tuple-element.33.active, bf16[128,512]{1,0:T(8,128)(2,1)S(1)} %collective-permute-done.6.part, bf16[128,1024]{1,0:T(8,128)(2,1)S(1)} %get-tuple-element.19.edges, ...), custom_call_target="tpu_custom_call" | custom-call | flops 671088640 | bytes 1048576 | tf_op jit(solution)/shard_map/pallas_call | solution.py:207
  25.8 1.4 %shard_map.38 = (f32[8,1280]{1,0:T(8,128)S(1)}, f32[8,1280]{1,0:T(8,128)S(1)}) custom-call(bf16[512,512]{1,0:T(8,128)(2,1)S(1)} %bitcast.10, bf16[8,128]{1,0:T(8,128)(2,1)S(1)} %get-tuple-element.33.active, bf16[128,1024]{1,0:T(8,128)(2,1)S(1)} %collective-permute-done.5.near, bf16[128,1024]{1,0:T(8,128)(2,1)S(1)} %get-tuple-element.19.edges, ...), custom_call_target="tpu_custom_call" | custom-call | flops 671088640 | bytes 1048576 | tf_op jit(solution)/shard_map/pallas_call | solution.py:179
  27.2 1.4 %shard_map.40 = (f32[16,2048]{1,0:T(8,128)S(1)}, f32[16,2048]{1,0:T(8,128)S(1)}) custom-call(s32[2]{0:T(128)S(1)} %pad_add_fusion.place, bf16[512,512]{1,0:T(8,128)(2,1)S(1)} %bitcast.11, bf16[8,128]{1,0:T(8,128)(2,1)S(1)} %get-tuple-element.33.active, bf16[128,512]{1,0:T(8,128)(2,1)S(1)} %collective-permute-done.3.part, ...), custom_call_target="tpu_custom_call" | custom-call | flops 268435456 | bytes 1048576 | tf_op jit(solution)/shard_map/pallas_call | solution.py:245
  28.6 0.1 collective-permute-start.7
  28.7 0.0 collective-permute-done
  28.7 0.1 broadcast_add_fusion
  28.8 1.5 %collective-permute-start.1 = (f32[16,128]{1,0:T(8,128)S(1)}, f32[16,128]{1,0:T(8,128)S(1)}, u32[]{:S(2)}, u32[]{:S(2)}) collective-permute-start(f32[16,128]{1,0:T(8,128)S(1)} %broadcast_add_fusion), channel_id=1, source_target_pairs={{0,2},{2,0},{1,3},{3,1},{4,6},{6,4},{5,7},{7,5},{8,10},{10,8},{9,1... | collective-permute-start | bytes 24584 | tf_op jit(solution)/shard_map/ppermute | solution.py:20
  30.3 0.0 collective-permute-done.7.refs_1_
  30.3 1.3 %collective-permute-start.8 = (f32[16,1024]{1,0:T(8,128)S(1)}, f32[16,1024]{1,0:T(8,128)S(1)}, u32[]{:S(2)}, u32[]{:S(2)}) collective-permute-start(f32[16,1024]{1,0:T(8,128)S(1)} %get-tuple-element.28), channel_id=1, source_target_pairs={{0,2},{2,0},{1,3},{3,1},{4,6},{6,4},{5,7},{7,5},{8,10},{10,8},{9,1... | collective-permute-start | bytes 196616 | tf_op jit(solution)/shard_map/ppermute | solution.py:20
  31.6 0.8 %collective-permute-done.1 = f32[16,128]{1,0:T(8,128)S(1)} collective-permute-done((f32[16,128]{1,0:T(8,128)S(1)}, f32[16,128]{1,0:T(8,128)S(1)}, u32[]{:S(2)}, u32[]{:S(2)}) %collective-permute-start.1) | collective-permute-done | bytes 8224 | tf_op jit(solution)/shard_map/ppermute | solution.py:20
  32.5 0.1 fusion.2.stats
  32.5 2.1 %collective-permute-done.8.refs_1_ = f32[16,1024]{1,0:T(8,128)S(1)} collective-permute-done((f32[16,1024]{1,0:T(8,128)S(1)}, f32[16,1024]{1,0:T(8,128)S(1)}, u32[]{:S(2)}, u32[]{:S(2)}) %collective-permute-start.8) | collective-permute-done | bytes 65568 | tf_op jit(solution)/shard_map/ppermute | solution.py:20
  34.7 0.1 shard_map.42
  34.8 1.4 %collective-permute-start.9 = (f32[8,1024]{1,0:T(8,128)S(1)}, f32[8,1024]{1,0:T(8,128)S(1)}, u32[]{:S(2)}, u32[]{:S(2)}) collective-permute-start(f32[8,1024]{1,0:T(8,128)S(1)} %shard_map.42), channel_id=1, source_target_pairs={{0,8},{1,12},{2,0},{3,4},{4,1},{5,13},{6,5},{7,9},{8,10},{9,14},{1... | collective-permute-start | bytes 98312 | tf_op jit(solution)/shard_map/ppermute | solution.py:461
  36.1 2.6 %collective-permute-done.9 = f32[8,1024]{1,0:T(8,128)S(1)} collective-permute-done((f32[8,1024]{1,0:T(8,128)S(1)}, f32[8,1024]{1,0:T(8,128)S(1)}, u32[]{:S(2)}, u32[]{:S(2)}) %collective-permute-start.9) | collective-permute-done | bytes 32800 | tf_op jit(solution)/shard_map/ppermute | solution.py:461
  38.7 0.6 %copy.8 = f32[8,1024]{1,0:T(8,128)} copy(f32[8,1024]{1,0:T(8,128)S(1)} %collective-permute-done.9) | data formatting | bytes 65536
  (10 shorter events, 0.0 us)
Async XLA Ops:
  0.0 7.9 %copy-start.1 = (bf16[8,128,256]{2,1,0:T(8,128)(2,1)S(1)}, bf16[8,128,256]{2,1,0:T(8,128)(2,1)}, u32[]{:S(2)}) copy-start(bf16[8,128,256]{2,1,0:T(8,128)(2,1)} %param.4) | copy-start | bytes 1572868
  0.0 25.8 %collective-permute-start.5 = (bf16[128,1024]{1,0:T(8,128)(2,1)}, bf16[128,1024]{1,0:T(8,128)(2,1)S(1)}, u32[]{:S(2)}, u32[]{:S(2)}) collective-permute-start(bf16[128,1024]{1,0:T(8,128)(2,1)} %own.1), channel_id=1, source_target_pairs={{0,4},{4,0},{8,12},{12,8},{1,5},{5,1},{9,13},{13,9},{2,6},{6,2},{1... | collective-permute-start | bytes 786440 | tf_op jit(solution)/shard_map/ppermute | solution.py:367
  4.1 14.8 %collective-permute-start.2 = (bf16[128,512]{1,0:T(8,128)(2,1)S(1)}, bf16[128,512]{1,0:T(8,128)(2,1)S(1)}, u32[]{:S(2)}, u32[]{:S(2)}) collective-permute-start(bf16[128,512]{1,0:T(8,128)(2,1)S(1)} %get-tuple-element.32), channel_id=1, source_target_pairs={{0,8},{4,12},{8,0},{12,4},{1,9},{5,13},{9,1},{13,5},{2,10},{6,14},... | collective-permute-start | bytes 393224 | tf_op jit(solution)/shard_map/ppermute | solution.py:367
  6.7 11.7 %collective-permute-start.4 = (bf16[128,512]{1,0:T(8,128)(2,1)S(1)}, bf16[128,512]{1,0:T(8,128)(2,1)S(1)}, u32[]{:S(2)}, u32[]{:S(2)}) collective-permute-start(bf16[128,512]{1,0:T(8,128)(2,1)S(1)} %get-tuple-element.31), channel_id=1, source_target_pairs={{0,8},{4,12},{8,0},{12,4},{1,9},{5,13},{9,1},{13,5},{2,10},{6,14},... | collective-permute-start | bytes 393224 | tf_op jit(solution)/shard_map/ppermute | solution.py:367
  8.6 20.1 %collective-permute-start = (f32[16,128]{1,0:T(8,128)S(1)}, f32[16,128]{1,0:T(8,128)S(1)}, u32[]{:S(2)}, u32[]{:S(2)}) collective-permute-start(f32[16,128]{1,0:T(8,128)S(1)} %broadcast_in_dim.6), channel_id=1, source_target_pairs={{0,1},{1,0},{2,3},{3,2},{4,5},{5,4},{6,7},{7,6},{8,9},{9,8},{10,11... | collective-permute-start | bytes 24584 | tf_op jit(solution)/shard_map/ppermute | solution.py:20
  18.4 6.0 %collective-permute-start.6 = (bf16[128,512]{1,0:T(8,128)(2,1)S(1)}, bf16[128,512]{1,0:T(8,128)(2,1)S(1)}, u32[]{:S(2)}, u32[]{:S(2)}) collective-permute-start(bf16[128,512]{1,0:T(8,128)(2,1)S(1)} %collective-permute-done.4.refs_0_), channel_id=1, source_target_pairs={{0,4},{4,0},{8,12},{12,8},{1,5},{5,1},{9,13},{13,9},{2,6},{6,2},{1... | collective-permute-start | bytes 393224 | tf_op jit(solution)/shard_map/ppermute | solution.py:367
  18.5 2.5 %copy-start = (bf16[128,1024]{1,0:T(8,128)(2,1)S(1)}, bf16[128,1024]{1,0:T(8,128)(2,1)}, u32[]{:S(2)}) copy-start(bf16[128,1024]{1,0:T(8,128)(2,1)} %own.1) | copy-start | bytes 786436
  18.9 8.3 %collective-permute-start.3 = (bf16[128,512]{1,0:T(8,128)(2,1)S(1)}, bf16[128,512]{1,0:T(8,128)(2,1)S(1)}, u32[]{:S(2)}, u32[]{:S(2)}) collective-permute-start(bf16[128,512]{1,0:T(8,128)(2,1)S(1)} %collective-permute-done.2.refs_1_), channel_id=1, source_target_pairs={{0,4},{4,0},{8,12},{12,8},{1,5},{5,1},{9,13},{13,9},{2,6},{6,2},{1... | collective-permute-start | bytes 393224 | tf_op jit(solution)/shard_map/ppermute | solution.py:367
  28.6 1.7 %collective-permute-start.7 = (f32[16,2048]{1,0:T(8,128)S(1)}, f32[16,2048]{1,0:T(8,128)S(1)}, u32[]{:S(2)}, u32[]{:S(2)}) collective-permute-start(f32[16,2048]{1,0:T(8,128)S(1)} %get-tuple-element.26), channel_id=1, source_target_pairs={{0,1},{1,0},{2,3},{3,2},{4,5},{5,4},{6,7},{7,6},{8,9},{9,8},{10,11... | collective-permute-start | bytes 393224 | tf_op jit(solution)/shard_map/ppermute | solution.py:20
  28.8 3.7 %collective-permute-start.1 = (f32[16,128]{1,0:T(8,128)S(1)}, f32[16,128]{1,0:T(8,128)S(1)}, u32[]{:S(2)}, u32[]{:S(2)}) collective-permute-start(f32[16,128]{1,0:T(8,128)S(1)} %broadcast_add_fusion), channel_id=1, source_target_pairs={{0,2},{2,0},{1,3},{3,1},{4,6},{6,4},{5,7},{7,5},{8,10},{10,8},{9,1... | collective-permute-start | bytes 24584 | tf_op jit(solution)/shard_map/ppermute | solution.py:20
  30.3 4.3 %collective-permute-start.8 = (f32[16,1024]{1,0:T(8,128)S(1)}, f32[16,1024]{1,0:T(8,128)S(1)}, u32[]{:S(2)}, u32[]{:S(2)}) collective-permute-start(f32[16,1024]{1,0:T(8,128)S(1)} %get-tuple-element.28), channel_id=1, source_target_pairs={{0,2},{2,0},{1,3},{3,1},{4,6},{6,4},{5,7},{7,5},{8,10},{10,8},{9,1... | collective-permute-start | bytes 196616 | tf_op jit(solution)/shard_map/ppermute | solution.py:20
  34.8 4.0 %collective-permute-start.9 = (f32[8,1024]{1,0:T(8,128)S(1)}, f32[8,1024]{1,0:T(8,128)S(1)}, u32[]{:S(2)}, u32[]{:S(2)}) collective-permute-start(f32[8,1024]{1,0:T(8,128)S(1)} %shard_map.42), channel_id=1, source_target_pairs={{0,8},{1,12},{2,0},{3,4},{4,1},{5,13},{6,5},{7,9},{8,10},{9,14},{1... | collective-permute-start | bytes 98312 | tf_op jit(solution)/shard_map/ppermute | solution.py:461

commit v3 on v2

--- a/solution.py
+++ b/solution.py
@@ -280,8 +280,12 @@
 def line_sums(values, span):
     reach = 1
     while reach < span:
-        values = values + jnp.concatenate([values[:, reach:], values[:, :reach]], 1)
-        reach *= 2
+        ways = 4 if 4 * reach <= span else 2
+        moved = [
+            jnp.concatenate([values[:, by * reach :], values[:, : by * reach]], 1) for by in range(1, ways)
+        ]
+        values = sum(moved, values)
+        reach *= ways
     return values
 
 

time: 39.6 us -> 39.5 us (level)
  no operation moved by 1% of the time
where the time goes in v3:
time: 39.5 us; the launch traced here: 39.3 us
  waiting for transfers between devices  16.9 us (43%)
  starting transfers between devices  12.4 us (31%)
  Pallas kernels  6.2 us (16%)
  local copies, waits for them, and re-layouts  2.31 us (6%)
  other arithmetic  1.45 us (4%)
    ppermute x5, waiting for transfers between devices, paired(): lax.ppermute(x, axis, [(i, i ^ bit) for i in range(lax.axis_size(axis))])  11.3 us
    ppermute x5, starting transfers between devices, paired(): lax.ppermute(x, axis, [(i, i ^ bit) for i in range(lax.axis_size(axis))])  8.13 us
    ppermute x4, waiting for transfers between devices, shifted(): return lax.ppermute(x, axis, [(i, (i + by) % count) for i in range(count)])  2.96 us
    ppermute x4, starting transfers between devices, shifted(): return lax.ppermute(x, axis, [(i, (i + by) % count) for i in range(count)])  2.87 us
    ppermute x1, waiting for transfers between devices, on_device(): received.append(lax.ppermute(block, ('tm', 'chan', 'sub'), pairs))  2.59 us
    pallas_call x1, Pallas kernels, outer_call(): pl.pallas_call(functools.partial(outer_kernel, span), out_shape=(shape, s...  2.01 us
    pallas_call x1, Pallas kernels, late_call(): pl.pallas_call(functools.partial(late_kernel, span, ways, table), out_sha...  1.42 us
    ppermute x1, starting transfers between devices, on_device(): received.append(lax.ppermute(block, ('tm', 'chan', 'sub'), pairs))  1.39 us
  transfers between devices with their start and end apart: 10, of which 5 were waited for; matrix products, arithmetic and copies ran while one was open for 8% of the time, Pallas kernels for 16%

profile of v3, /device:TPU:0, one launch (start us, length us, event | category | flops | bytes accessed | tf_op | source)
XLA Modules:
  0.0 39.3 jit_solution(15590939482963719629)
XLA Ops:
  0.0 3.1 %collective-permute-start.5 = (bf16[128,1024]{1,0:T(8,128)(2,1)}, bf16[128,1024]{1,0:T(8,128)(2,1)S(1)}, u32[]{:S(2)}, u32[]{:S(2)}) collective-permute-start(bf16[128,1024]{1,0:T(8,128)(2,1)} %own.1), channel_id=1, source_target_pairs={{0,4},{4,0},{8,12},{12,8},{1,5},{5,1},{9,13},{13,9},{2,6},{6,2},{1... | collective-permute-start | bytes 786440 | tf_op jit(solution)/shard_map/ppermute | solution.py:371
  3.1 1.0 %fusion = (bf16[128,512]{1,0:T(8,128)(2,1)S(1)}, bf16[128,512]{1,0:T(8,128)(2,1)S(1)}) fusion(bf16[128,1024]{1,0:T(8,128)(2,1)} %own.1), kind=kLoop, calls=%fused_computation.5 | loop fusion | bytes 524288 | tf_op jit(solution)/shard_map/slice | solution.py:380
  4.1 2.7 %collective-permute-start.2 = (bf16[128,512]{1,0:T(8,128)(2,1)S(1)}, bf16[128,512]{1,0:T(8,128)(2,1)S(1)}, u32[]{:S(2)}, u32[]{:S(2)}) collective-permute-start(bf16[128,512]{1,0:T(8,128)(2,1)S(1)} %get-tuple-element.32), channel_id=1, source_target_pairs={{0,8},{4,12},{8,0},{12,4},{1,9},{5,13},{9,1},{13,5},{2,10},{6,14},... | collective-permute-start | bytes 393224 | tf_op jit(solution)/shard_map/ppermute | solution.py:371
  6.7 0.3 collective-permute-start.4
  7.0 0.9 %fusion.1 = (bf16[8,128]{1,0:T(8,128)(2,1)S(1)}, s32[8]{0:T(128)S(1)}) fusion(s32[8,128]{1,0:T(8,128)} %param.5), kind=kLoop, calls=%fused_computation.6 | loop fusion | flops 2040 | bytes 6176 | tf_op jit(solution)/shard_map/convert_element_type | solution.py:428
  7.9 0.3 copy.5
  8.2 0.3 multiply_reduce_fusion
  8.5 0.1 pad_maximum_fusion
  8.6 0.1 broadcast_in_dim.6
  8.6 9.8 %collective-permute-done.4.refs_0_ = bf16[128,512]{1,0:T(8,128)(2,1)S(1)} collective-permute-done((bf16[128,512]{1,0:T(8,128)(2,1)S(1)}, bf16[128,512]{1,0:T(8,128)(2,1)S(1)}, u32[]{:S(2)}, u32[]{:S(2)}) %collective-permute-start.4) | collective-permute-done | bytes 131104 | tf_op jit(solution)/shard_map/ppermute | solution.py:371
  18.4 0.1 pad_add_fusion.place
  18.5 0.3 copy.6
  18.9 0.0 collective-permute-done.2.refs_1_
  18.9 2.1 %collective-permute-start.3 = (bf16[128,512]{1,0:T(8,128)(2,1)S(1)}, bf16[128,512]{1,0:T(8,128)(2,1)S(1)}, u32[]{:S(2)}, u32[]{:S(2)}) collective-permute-start(bf16[128,512]{1,0:T(8,128)(2,1)S(1)} %collective-permute-done.2.refs_1_), channel_id=1, source_target_pairs={{0,4},{4,0},{8,12},{12,8},{1,5},{5,1},{9,13},{13,9},{2,6},{6,2},{1... | collective-permute-start | bytes 393224 | tf_op jit(solution)/shard_map/ppermute | solution.py:371
  21.0 2.0 %shard_map.37 = (f32[8,1536]{1,0:T(8,128)S(1)}, f32[8,1536]{1,0:T(8,128)S(1)}, bf16[128,1024]{1,0:T(8,128)(2,1)S(1)}, f32[8,1024]{1,0:T(8,128)S(1)}) custom-call(s32[1]{0:T(128)} %bitcast.6.odd, bf16[512,512]{1,0:T(8,128)(2,1)S(1)} %bitcast.8, bf16[8,128]{1,0:T(8,128)(2,1)S(1)} %get-tuple-element.33.active, bf16[128,1024]{1,0:T(8,128)(2,1)S(1)} %copy-done, ...), custom_call_target="tpu_custom_call" | custom-call | flops 805306368 | bytes 1048576 | tf_op jit(solution)/shard_map/pallas_call | solution.py:148
  23.0 1.5 %collective-permute-done.6.part = bf16[128,512]{1,0:T(8,128)(2,1)S(1)} collective-permute-done((bf16[128,512]{1,0:T(8,128)(2,1)S(1)}, bf16[128,512]{1,0:T(8,128)(2,1)S(1)}, u32[]{:S(2)}, u32[]{:S(2)}) %collective-permute-start.6) | collective-permute-done | bytes 131104 | tf_op jit(solution)/shard_map/ppermute | solution.py:371
  24.5 1.3 %shard_map.39 = (f32[8,1280]{1,0:T(8,128)S(1)}, f32[8,1280]{1,0:T(8,128)S(1)}) custom-call(bf16[512,512]{1,0:T(8,128)(2,1)S(1)} %bitcast.9, bf16[8,128]{1,0:T(8,128)(2,1)S(1)} %get-tuple-element.33.active, bf16[128,512]{1,0:T(8,128)(2,1)S(1)} %collective-permute-done.6.part, bf16[128,1024]{1,0:T(8,128)(2,1)S(1)} %get-tuple-element.19.edges, ...), custom_call_target="tpu_custom_call" | custom-call | flops 671088640 | bytes 1048576 | tf_op jit(solution)/shard_map/pallas_call | solution.py:207
  25.8 1.4 %shard_map.38 = (f32[8,1280]{1,0:T(8,128)S(1)}, f32[8,1280]{1,0:T(8,128)S(1)}) custom-call(bf16[512,512]{1,0:T(8,128)(2,1)S(1)} %bitcast.10, bf16[8,128]{1,0:T(8,128)(2,1)S(1)} %get-tuple-element.33.active, bf16[128,1024]{1,0:T(8,128)(2,1)S(1)} %collective-permute-done.5.near, bf16[128,1024]{1,0:T(8,128)(2,1)S(1)} %get-tuple-element.19.edges, ...), custom_call_target="tpu_custom_call" | custom-call | flops 671088640 | bytes 1048576 | tf_op jit(solution)/shard_map/pallas_call | solution.py:179
  27.2 0.0 collective-permute-done.3.part
  27.2 1.4 %shard_map.40 = (f32[16,2048]{1,0:T(8,128)S(1)}, f32[16,2048]{1,0:T(8,128)S(1)}) custom-call(s32[2]{0:T(128)S(1)} %pad_add_fusion.place, bf16[512,512]{1,0:T(8,128)(2,1)S(1)} %bitcast.11, bf16[8,128]{1,0:T(8,128)(2,1)S(1)} %get-tuple-element.33.active, bf16[128,512]{1,0:T(8,128)(2,1)S(1)} %collective-permute-done.3.part, ...), custom_call_target="tpu_custom_call" | custom-call | flops 268435456 | bytes 1048576 | tf_op jit(solution)/shard_map/pallas_call | solution.py:245
  28.6 0.1 collective-permute-start.7
  28.7 0.1 broadcast_add_fusion
  28.8 1.5 %collective-permute-start.1 = (f32[16,128]{1,0:T(8,128)S(1)}, f32[16,128]{1,0:T(8,128)S(1)}, u32[]{:S(2)}, u32[]{:S(2)}) collective-permute-start(f32[16,128]{1,0:T(8,128)S(1)} %broadcast_add_fusion), channel_id=1, source_target_pairs={{0,2},{2,0},{1,3},{3,1},{4,6},{6,4},{5,7},{7,5},{8,10},{10,8},{9,1... | collective-permute-start | bytes 24584 | tf_op jit(solution)/shard_map/ppermute | solution.py:20
  30.3 0.0 collective-permute-done.7.refs_1_
  30.3 1.3 %collective-permute-start.8 = (f32[16,1024]{1,0:T(8,128)S(1)}, f32[16,1024]{1,0:T(8,128)S(1)}, u32[]{:S(2)}, u32[]{:S(2)}) collective-permute-start(f32[16,1024]{1,0:T(8,128)S(1)} %get-tuple-element.28), channel_id=1, source_target_pairs={{0,2},{2,0},{1,3},{3,1},{4,6},{6,4},{5,7},{7,5},{8,10},{10,8},{9,1... | collective-permute-start | bytes 196616 | tf_op jit(solution)/shard_map/ppermute | solution.py:20
  31.6 0.8 %collective-permute-done.1 = f32[16,128]{1,0:T(8,128)S(1)} collective-permute-done((f32[16,128]{1,0:T(8,128)S(1)}, f32[16,128]{1,0:T(8,128)S(1)}, u32[]{:S(2)}, u32[]{:S(2)}) %collective-permute-start.1) | collective-permute-done | bytes 8224 | tf_op jit(solution)/shard_map/ppermute | solution.py:20
  32.4 0.1 fusion.2.stats
  32.5 2.1 %collective-permute-done.8.refs_1_ = f32[16,1024]{1,0:T(8,128)S(1)} collective-permute-done((f32[16,1024]{1,0:T(8,128)S(1)}, f32[16,1024]{1,0:T(8,128)S(1)}, u32[]{:S(2)}, u32[]{:S(2)}) %collective-permute-start.8) | collective-permute-done | bytes 65568 | tf_op jit(solution)/shard_map/ppermute | solution.py:20
  34.6 0.1 shard_map.42
  34.7 1.4 %collective-permute-start.9 = (f32[8,1024]{1,0:T(8,128)S(1)}, f32[8,1024]{1,0:T(8,128)S(1)}, u32[]{:S(2)}, u32[]{:S(2)}) collective-permute-start(f32[8,1024]{1,0:T(8,128)S(1)} %shard_map.42), channel_id=1, source_target_pairs={{0,8},{1,12},{2,0},{3,4},{4,1},{5,13},{6,5},{7,9},{8,10},{9,14},{1... | collective-permute-start | bytes 98312 | tf_op jit(solution)/shard_map/ppermute | solution.py:465
  36.1 2.6 %collective-permute-done.9 = f32[8,1024]{1,0:T(8,128)S(1)} collective-permute-done((f32[8,1024]{1,0:T(8,128)S(1)}, f32[8,1024]{1,0:T(8,128)S(1)}, u32[]{:S(2)}, u32[]{:S(2)}) %collective-permute-start.9) | collective-permute-done | bytes 32800 | tf_op jit(solution)/shard_map/ppermute | solution.py:465
  38.7 0.6 %copy.8 = f32[8,1024]{1,0:T(8,128)} copy(f32[8,1024]{1,0:T(8,128)S(1)} %collective-permute-done.9) | data formatting | bytes 65536
  (10 shorter events, 0.0 us)
Async XLA Ops:
  0.0 7.9 %copy-start.1 = (bf16[8,128,256]{2,1,0:T(8,128)(2,1)S(1)}, bf16[8,128,256]{2,1,0:T(8,128)(2,1)}, u32[]{:S(2)}) copy-start(bf16[8,128,256]{2,1,0:T(8,128)(2,1)} %param.4) | copy-start | bytes 1572868
  0.0 25.8 %collective-permute-start.5 = (bf16[128,1024]{1,0:T(8,128)(2,1)}, bf16[128,1024]{1,0:T(8,128)(2,1)S(1)}, u32[]{:S(2)}, u32[]{:S(2)}) collective-permute-start(bf16[128,1024]{1,0:T(8,128)(2,1)} %own.1), channel_id=1, source_target_pairs={{0,4},{4,0},{8,12},{12,8},{1,5},{5,1},{9,13},{13,9},{2,6},{6,2},{1... | collective-permute-start | bytes 786440 | tf_op jit(solution)/shard_map/ppermute | solution.py:371
  4.1 14.8 %collective-permute-start.2 = (bf16[128,512]{1,0:T(8,128)(2,1)S(1)}, bf16[128,512]{1,0:T(8,128)(2,1)S(1)}, u32[]{:S(2)}, u32[]{:S(2)}) collective-permute-start(bf16[128,512]{1,0:T(8,128)(2,1)S(1)} %get-tuple-element.32), channel_id=1, source_target_pairs={{0,8},{4,12},{8,0},{12,4},{1,9},{5,13},{9,1},{13,5},{2,10},{6,14},... | collective-permute-start | bytes 393224 | tf_op jit(solution)/shard_map/ppermute | solution.py:371
  6.7 11.7 %collective-permute-start.4 = (bf16[128,512]{1,0:T(8,128)(2,1)S(1)}, bf16[128,512]{1,0:T(8,128)(2,1)S(1)}, u32[]{:S(2)}, u32[]{:S(2)}) collective-permute-start(bf16[128,512]{1,0:T(8,128)(2,1)S(1)} %get-tuple-element.31), channel_id=1, source_target_pairs={{0,8},{4,12},{8,0},{12,4},{1,9},{5,13},{9,1},{13,5},{2,10},{6,14},... | collective-permute-start | bytes 393224 | tf_op jit(solution)/shard_map/ppermute | solution.py:371
  8.6 20.0 %collective-permute-start = (f32[16,128]{1,0:T(8,128)S(1)}, f32[16,128]{1,0:T(8,128)S(1)}, u32[]{:S(2)}, u32[]{:S(2)}) collective-permute-start(f32[16,128]{1,0:T(8,128)S(1)} %broadcast_in_dim.6), channel_id=1, source_target_pairs={{0,1},{1,0},{2,3},{3,2},{4,5},{5,4},{6,7},{7,6},{8,9},{9,8},{10,11... | collective-permute-start | bytes 24584 | tf_op jit(solution)/shard_map/ppermute | solution.py:20
  18.4 6.0 %collective-permute-start.6 = (bf16[128,512]{1,0:T(8,128)(2,1)S(1)}, bf16[128,512]{1,0:T(8,128)(2,1)S(1)}, u32[]{:S(2)}, u32[]{:S(2)}) collective-permute-start(bf16[128,512]{1,0:T(8,128)(2,1)S(1)} %collective-permute-done.4.refs_0_), channel_id=1, source_target_pairs={{0,4},{4,0},{8,12},{12,8},{1,5},{5,1},{9,13},{13,9},{2,6},{6,2},{1... | collective-permute-start | bytes 393224 | tf_op jit(solution)/shard_map/ppermute | solution.py:371
  18.5 2.5 %copy-start = (bf16[128,1024]{1,0:T(8,128)(2,1)S(1)}, bf16[128,1024]{1,0:T(8,128)(2,1)}, u32[]{:S(2)}) copy-start(bf16[128,1024]{1,0:T(8,128)(2,1)} %own.1) | copy-start | bytes 786436
  18.9 8.3 %collective-permute-start.3 = (bf16[128,512]{1,0:T(8,128)(2,1)S(1)}, bf16[128,512]{1,0:T(8,128)(2,1)S(1)}, u32[]{:S(2)}, u32[]{:S(2)}) collective-permute-start(bf16[128,512]{1,0:T(8,128)(2,1)S(1)} %collective-permute-done.2.refs_1_), channel_id=1, source_target_pairs={{0,4},{4,0},{8,12},{12,8},{1,5},{5,1},{9,13},{13,9},{2,6},{6,2},{1... | collective-permute-start | bytes 393224 | tf_op jit(solution)/shard_map/ppermute | solution.py:371
  28.6 1.7 %collective-permute-start.7 = (f32[16,2048]{1,0:T(8,128)S(1)}, f32[16,2048]{1,0:T(8,128)S(1)}, u32[]{:S(2)}, u32[]{:S(2)}) collective-permute-start(f32[16,2048]{1,0:T(8,128)S(1)} %get-tuple-element.26), channel_id=1, source_target_pairs={{0,1},{1,0},{2,3},{3,2},{4,5},{5,4},{6,7},{7,6},{8,9},{9,8},{10,11... | collective-permute-start | bytes 393224 | tf_op jit(solution)/shard_map/ppermute | solution.py:20
  28.8 3.7 %collective-permute-start.1 = (f32[16,128]{1,0:T(8,128)S(1)}, f32[16,128]{1,0:T(8,128)S(1)}, u32[]{:S(2)}, u32[]{:S(2)}) collective-permute-start(f32[16,128]{1,0:T(8,128)S(1)} %broadcast_add_fusion), channel_id=1, source_target_pairs={{0,2},{2,0},{1,3},{3,1},{4,6},{6,4},{5,7},{7,5},{8,10},{10,8},{9,1... | collective-permute-start | bytes 24584 | tf_op jit(solution)/shard_map/ppermute | solution.py:20
  30.3 4.3 %collective-permute-start.8 = (f32[16,1024]{1,0:T(8,128)S(1)}, f32[16,1024]{1,0:T(8,128)S(1)}, u32[]{:S(2)}, u32[]{:S(2)}) collective-permute-start(f32[16,1024]{1,0:T(8,128)S(1)} %get-tuple-element.28), channel_id=1, source_target_pairs={{0,2},{2,0},{1,3},{3,1},{4,6},{6,4},{5,7},{7,5},{8,10},{10,8},{9,1... | collective-permute-start | bytes 196616 | tf_op jit(solution)/shard_map/ppermute | solution.py:20
  34.7 4.0 %collective-permute-start.9 = (f32[8,1024]{1,0:T(8,128)S(1)}, f32[8,1024]{1,0:T(8,128)S(1)}, u32[]{:S(2)}, u32[]{:S(2)}) collective-permute-start(f32[8,1024]{1,0:T(8,128)S(1)} %shard_map.42), channel_id=1, source_target_pairs={{0,8},{1,12},{2,0},{3,4},{4,1},{5,13},{6,5},{7,9},{8,10},{9,14},{1... | collective-permute-start | bytes 98312 | tf_op jit(solution)/shard_map/ppermute | solution.py:465
